TPU v7x, 512 devices: a whole 4x4x16 slice. The times are simulated.
512 devices in a mesh: rows: 8 (over x_lo, y), cols: 64 (over z, x_hi, core).
Axes of the slice: x: 4 (x_hi: 2, x_lo: 2; x = x_hi * 2 + x_lo), y: 4, z: 16, core: 2. Of those that a mesh axis runs over, the one named last changes fastest.
Arguments:
- points: bfloat16 [32, 16384], P(None, ('rows', 'cols')), may hold values from 0 to 1
- samples: bfloat16 [32, 32768], P(None, 'cols'), may hold values from -0.5 to 1.5
- potential: float32 [32768], P('cols'), may hold values from -6 to 60
Outputs:
- point_potential: float32 [16384], P(('rows', 'cols'))
- sample_potential: float32 [32768], P('cols')
- barycenter: float32 [32, 16384], P(None, ('rows', 'cols'))
All inputs are finite; a program needn't handle non-finite values.
Results may differ from a plain program's by a relative error of at most 0.00055.
Values may be sent and summed in bfloat16 or wider, within the bound.
No kernel may reach another device: no remote copies, remote signals or barrier semaphores. Data moves between devices by JAX's collectives and lax.ppermute only.
A program may use at most 64 MiB of HBM per device.

v0:
```python
import math

import jax
import jax.numpy as jnp
from jax import lax
from jax.sharding import PartitionSpec as P

EPS = 0.25


def joined(part, axis, combine):
    gathered = jax.tree.map(lambda a: lax.all_gather(a, axis), part)

    def take(source):
        return jax.tree.map(lambda a: lax.dynamic_index_in_dim(a, source, 0, False), gathered)

    return lax.fori_loop(
        1, lax.axis_size(axis), lambda source, state: combine(state, take(source)), take(0)
    )


def combine_stats(first, second):
    top = jnp.maximum(first[0], second[0])
    total = first[1] * jnp.exp(first[0] - top) + second[1] * jnp.exp(second[0] - top)
    return (top, total)


def on_device(points, samples, potential):
    own_count = points.shape[1]
    whole = lax.all_gather(points, "cols", axis=1, tiled=True)
    block_count = whole.shape[1]
    col_count = lax.axis_size("cols")
    total_samples = samples.shape[1] * col_count
    total_points = block_count * lax.axis_size("rows")
    xf = whole.astype(jnp.float32)
    yf = samples.astype(jnp.float32)
    point_sq = jnp.sum(xf * xf, axis=0)
    sample_sq = jnp.sum(yf * yf, axis=0)
    cross = lax.dot_general(
        whole, samples, (((0,), (0,)), ((), ())), preferred_element_type=jnp.float32
    )
    cost = 0.5 * point_sq[:, None] + 0.5 * sample_sq[None, :] - cross
    score = (potential[None, :] - cost) / EPS
    row_top = lax.pmax(jnp.max(score, axis=1), "cols")
    row_sum = lax.psum(jnp.sum(jnp.exp(score - row_top[:, None]), axis=1), "cols")
    point_full = -EPS * (row_top + jnp.log(row_sum) - math.log(total_samples))
    col_score = (point_full[:, None] - cost) / EPS
    col_top = jnp.max(col_score, axis=0)
    col_sum = jnp.sum(jnp.exp(col_score - col_top[None, :]), axis=0)
    col_top, col_sum = joined((col_top, col_sum), "rows", combine_stats)
    sample_potential = -EPS * (col_top + jnp.log(col_sum) - math.log(total_points))
    new_score = (sample_potential[None, :] - cost) / EPS
    block_top = jnp.max(new_score, axis=1)
    weight = jnp.exp(new_score - block_top[:, None]).astype(jnp.bfloat16)
    denom = jnp.sum(weight.astype(jnp.float32), axis=1)
    numer = lax.dot_general(
        samples, weight, (((1,), (1,)), ((), ())), preferred_element_type=jnp.float32
    )
    position = lax.axis_index("cols") * own_count
    new_top = lax.pmax(block_top, "cols")
    scale = jnp.exp(block_top - new_top)
    numer_scaled = numer * scale[None, :]
    denom_scaled = denom * scale
    numer_all, denom_all = lax.psum((numer_scaled, denom_scaled), "cols")
    numer_own = lax.dynamic_slice_in_dim(numer_all, position, own_count, 1)
    denom_own = lax.dynamic_slice_in_dim(denom_all, position, own_count, 0)
    barycenter = numer_own / denom_own[None, :]
    point_potential = lax.dynamic_slice_in_dim(point_full, position, own_count, 0)
    return (point_potential, sample_potential, barycenter)


def solution(mesh):
    placed = (P(None, ("rows", "cols")), P(None, "cols"), P("cols"))
    return jax.shard_map(
        on_device,
        mesh=mesh,
        in_specs=placed,
        out_specs=(P(("rows", "cols")), P("cols"), P(None, ("rows", "cols"))),
        check_vma=False,
    )
```

profile of v0, /device:TPU:1, one launch (start us, length us, event | category | flops | bytes accessed | tf_op | source)
XLA Modules:
  0.0 1036.2 jit_solution(15728335356451031905)
XLA Ops:
  7.2 0.0 copy-start.4
  7.2 0.0 all-reduce.2.cloned.1.call-start
  7.2 0.8 multiply_reduce_fusion.1
  8.0 0.8 copy.6
  8.8 86.0 %all_gather.15 = bf16[32,2048]{0,1:T(8,128)(2,1)S(1)} all-gather(bf16[32,32]{0,1:T(8,128)(2,1)S(1)} %copy.6), channel_id=1, replica_groups=mesh['rows'=8,'cols'=64] {'cols'}, dimensions={1}, use_global_device_ids=true | all-gather | bytes 133120 | tf_op jit(solution)/shard_map/all_gather | solution.py:30
  94.8 0.3 multiply_reduce_fusion
  95.2 3.6 fusion
  98.8 130.3 %pmax.14 = f32[2048]{0:T(1024)S(1)} all-reduce(f32[2048]{0:T(1024)S(1)} %get-tuple-element.156), channel_id=1, replica_groups=mesh['rows'=8,'cols'=64] {'cols'}, use_global_device_ids=true, to_apply=%region_3.0 | all-reduce | flops 2048 | bytes 16384 | tf_op jit(solution)/shard_map/pmax | solution.py:44
  229.1 0.0 copy-done.4
  229.1 3.1 exponential_reduce_fusion.1
  232.2 131.1 %psum.21 = f32[2048]{0:T(1024)S(1)} all-reduce(f32[2048]{0:T(1024)S(1)} %exponential_reduce_fusion.1), channel_id=1, replica_groups=mesh['rows'=8,'cols'=64] {'cols'}, use_global_device_ids=true, to_apply=%region_5.0 | all-reduce | flops 2048 | bytes 16384 | tf_op jit(solution)/shard_map/psum | solution.py:45
  363.4 0.0 copy-start
  363.4 2.8 fusion.1
  366.2 0.6 copy-done
  366.8 0.9 exponential_reduce_fusion
  367.7 19.0 %all-gather.2 = f32[8,1,512]{2,1,0:T(1,128)S(1)} all-gather(f32[1,1,512]{2,1,0:T(1,128)S(1)} %bitcast.28), channel_id=2, replica_groups=mesh['rows'=8,'cols'=64] {'rows'}, dimensions={0}, use_global_device_ids=true | all-gather | bytes 18432 | tf_op jit(solution)/shard_map/all_gather | solution.py:12
  386.8 19.0 %all-gather.3 = f32[8,1,512]{2,1,0:T(1,128)S(1)} all-gather(f32[1,1,512]{2,1,0:T(1,128)S(1)} %bitcast.29), channel_id=3, replica_groups=mesh['rows'=8,'cols'=64] {'rows'}, dimensions={0}, use_global_device_ids=true | all-gather | bytes 18432 | tf_op jit(solution)/shard_map/all_gather | solution.py:12
  405.8 0.4 while.17
  406.2 0.0 copy-start.1
  406.2 0.0 copy-start.3
  406.3 2.8 fusion.2
  409.1 0.6 copy-done.1
  409.7 0.0 copy-start.2
  409.7 1.1 convert_reduce_fusion
  410.8 0.0 copy-done.3
  410.8 140.0 %pmax.15 = f32[2048]{0:T(1024)S(1)} all-reduce(f32[2048]{0:T(1024)S(1)} %fusion.2), channel_id=1, replica_groups=mesh['rows'=8,'cols'=64] {'cols'}, use_global_device_ids=true, to_apply=%region_11.12 | all-reduce | flops 2048 | bytes 16384 | tf_op jit(solution)/shard_map/pmax | solution.py:60
  550.8 0.0 copy-done.2
  550.8 1.2 fusion.3
  552.0 0.0 all-reduce.2.cloned.1.call-update
  552.0 0.6 dynamic_slice.36
  552.6 130.8 %psum.23 = f32[2048]{0:T(1024)S(1)} all-reduce(f32[2048]{0:T(1024)S(1)} %get-tuple-element.150), channel_id=1, replica_groups=mesh['rows'=8,'cols'=64] {'cols'}, use_global_device_ids=true, to_apply=%region_14.15 | all-reduce | flops 2048 | bytes 16384 | tf_op jit(solution)/shard_map/psum | solution.py:64
  683.4 0.1 dynamic_slice.40
  683.5 344.5 %all-reduce.2.cloned.1.call-done = f32[32,2048]{1,0:T(8,128)} async-done(((f32[32,2048]{1,0:T(8,128)}), f32[32,2048]{1,0:T(8,128)}) %all-reduce.2.cloned.1.call-update) | async-done | bytes 262160 | tf_op jit(solution)/shard_map/psum | solution.py:64
  1028.0 1.4 dynamic-slice_divide_fusion
  (23 shorter events, 0.3 us)
Async XLA Ops:
  7.2 221.9 %copy-start.4 = (f32[512]{0:T(512)S(1)}, f32[512]{0:T(512)}, u32[]{:S(2)}) copy-start(f32[512]{0:T(512)} %param.7) | copy-start | bytes 6148
  7.2 1020.8 %all-reduce.2.cloned.1.call-start = ((), (), s32[]{:S(2)}) async-start(), calls=%async_computation | async-start | bytes 524288 | tf_op jit(solution)/shard_map/psum | solution.py:64
  363.4 3.5 copy-start
  406.2 3.5 copy-start.1
  406.2 4.5 copy-start.3
  409.7 141.1 %copy-start.2 = (bf16[32,512]{1,0:T(8,128)(2,1)S(1)}, bf16[32,512]{1,0:T(8,128)(2,1)}, u32[]{:S(2)}) copy-start(bf16[32,512]{1,0:T(8,128)(2,1)} %param.6) | copy-start | bytes 98308
Sparse Core Ops, SparseCore 0:
  552.1 475.8 all-reduce.1
where the time goes:
time: 1040 us
  blocking collectives  656 us (63%)
  waiting for transfers between devices  345 us (33%)
  between operations  14.2 us (1%)
  other arithmetic  13.5 us (1%)
    psum x1, waiting for transfers between devices, on_device(): numer_all, denom_all = lax.psum((numer_scaled, denom_scaled), 'cols')  344 us
    pmax x1, blocking collectives, on_device(): new_top = lax.pmax(block_top, 'cols')  140 us
    psum x1, blocking collectives, on_device(): lax.psum(jnp.sum(jnp.exp(score - row_top[:, None]), axis=1), 'cols')  131 us
    psum x1, blocking collectives, on_device(): numer_all, denom_all = lax.psum((numer_scaled, denom_scaled), 'cols')  131 us
    pmax x1, blocking collectives, on_device(): row_top = lax.pmax(jnp.max(score, axis=1), 'cols')  130 us
    all_gather x1, blocking collectives, on_device(): whole = lax.all_gather(points, 'cols', axis=1, tiled=True)  86 us
    all_gather x2, blocking collectives, joined(): gathered = jax.tree.map(lambda a: lax.all_gather(a, axis), part)  38.1 us
  transfers between devices with their start and end apart: 1, of which 1 were waited for; matrix products, arithmetic and copies ran while one was open for 0% of the time, Pallas kernels for 0%

commit v1 on v0

v1 whole, which is shorter than its diff:
```python
import math

import jax
import jax.numpy as jnp
from jax import lax
from jax.sharding import PartitionSpec as P

EPS = 0.25


def spread(part, axis):
    count = lax.axis_size(axis)
    return lax.all_to_all(jnp.broadcast_to(part, (count,) + part.shape), axis, 0, 0)


def combine(lse):
    top = jnp.max(lse, axis=0)
    return top + jnp.log(jnp.sum(jnp.exp(lse - top[None]), axis=0))


def on_device(points, samples, potential):
    own_count = points.shape[1]
    dim = points.shape[0]
    col_count = lax.axis_size("cols")
    block_count = own_count * col_count
    sample_count = samples.shape[1]
    total_samples = sample_count * col_count
    total_points = block_count * lax.axis_size("rows")
    whole = spread(points.T, "cols").reshape(block_count, dim)
    xf = whole.astype(jnp.float32)
    yf = samples.astype(jnp.float32)
    point_sq = jnp.sum(xf * xf, axis=1)
    sample_sq = jnp.sum(yf * yf, axis=0)
    cross = lax.dot_general(
        whole, samples, (((1,), (0,)), ((), ())), preferred_element_type=jnp.float32
    )
    cost = 0.5 * point_sq[:, None] + 0.5 * sample_sq[None, :] - cross
    score = (potential[None, :] - cost) / EPS
    row_top = jnp.max(score, axis=1)
    row_lse = row_top + jnp.log(jnp.sum(jnp.exp(score - row_top[:, None]), axis=1))
    own_lse = combine(lax.all_to_all(row_lse.reshape(col_count, own_count), "cols", 0, 0))
    point_potential = -EPS * (own_lse - math.log(total_samples))
    point_full = spread(point_potential, "cols").reshape(block_count)
    col_score = (point_full[:, None] - cost) / EPS
    col_top = jnp.max(col_score, axis=0)
    col_lse = col_top + jnp.log(jnp.sum(jnp.exp(col_score - col_top[None, :]), axis=0))
    col_lse = combine(spread(col_lse, "rows"))
    sample_potential = -EPS * (col_lse - math.log(total_points))
    new_score = (sample_potential[None, :] - cost) / EPS
    block_top = jnp.max(new_score, axis=1)
    weight = jnp.exp(new_score - block_top[:, None]).astype(jnp.bfloat16)
    denom = jnp.sum(weight.astype(jnp.float32), axis=1)
    numer = lax.dot_general(
        weight, samples, (((1,), (1,)), ((), ())), preferred_element_type=jnp.float32
    )
    parts = jnp.concatenate([numer, denom[:, None], block_top[:, None]], axis=1)
    parts = parts.reshape(col_count, own_count * (dim + 2))
    parts = lax.all_to_all(parts, "cols", 0, 0).reshape(col_count, own_count, dim + 2)
    top = parts[:, :, dim + 1]
    scale = jnp.exp(top - jnp.max(top, axis=0)[None])
    total = jnp.sum(parts[:, :, : dim + 1] * scale[:, :, None], axis=0)
    barycenter = (total[:, :dim] / total[:, dim:]).T
    return (point_potential, sample_potential, barycenter)


def solution(mesh):
    placed = (P(None, ("rows", "cols")), P(None, "cols"), P("cols"))
    return jax.shard_map(
        on_device,
        mesh=mesh,
        in_specs=placed,
        out_specs=(P(("rows", "cols")), P("cols"), P(None, ("rows", "cols"))),
        check_vma=False,
    )
```

time: 1040 us -> 138 us (0.13)
  blocking collectives: 656 us -> 76.6 us
  waiting for transfers between devices: 345 us -> 17.8 us
  starting transfers between devices: 0.04 us -> 19.6 us
  between operations: 14.2 us -> 0.89 us
    psum x1 -> x0, waiting for transfers between devices: 344 us -> none  [on_device(): numer_all, denom_all = lax.psum((numer_scaled, denom_scaled), 'cols')]
    pmax x2 -> x0, blocking collectives: 270 us -> none  [the longest x1 140 us: on_device(): new_top = lax.pmax(block_top, 'cols')]
    psum x2 -> x0, blocking collectives: 262 us -> none  [the longest x1 131 us: on_device(): lax.psum(jnp.sum(jnp.exp(score - row_top[:, None]), axis=1), 'cols')]
    all_gather x3 -> x0, blocking collectives: 124 us -> none  [the longest x1 86 us: on_device(): whole = lax.all_gather(points, 'cols', axis=1, tiled=True)]
    all_to_all x0 -> x4, blocking collectives: none -> 76.6 us  [the longest x1 30.4 us: on_device(): lax.all_to_all(parts, 'cols', 0, 0).reshape(col_count, own_count, dim + 2)]
    all_to_all x0 -> x1, starting transfers between devices: none -> 19.6 us  [spread(): lax.all_to_all(jnp.broadcast_to(part, (count,) + part.shape), axis, 0, 0)]
    all_to_all x0 -> x1, waiting for transfers between devices: none -> 17.8 us  [spread(): lax.all_to_all(jnp.broadcast_to(part, (count,) + part.shape), axis, 0, 0)]
  transfers between devices with their start and end apart: 1 -> 1, of which waited for: 1 -> 1; matrix products, arithmetic and copies ran while one was open for 0% -> 1% of each run, Pallas kernels for 0% -> 0%
where the time goes in v1:
time: 138 us
  blocking collectives  76.6 us (56%)
  starting transfers between devices  19.6 us (14%)
  waiting for transfers between devices  17.8 us (13%)
  other arithmetic  11.2 us (8%)
  local copies, waits for them, and re-layouts  10.3 us (7%)
  matrix products  1.44 us (1%)
    all_to_all x1, blocking collectives, on_device(): lax.all_to_all(parts, 'cols', 0, 0).reshape(col_count, own_count, dim + 2)  30.4 us
    all_to_all x2, blocking collectives, spread(): lax.all_to_all(jnp.broadcast_to(part, (count,) + part.shape), axis, 0, 0)  27.7 us
    all_to_all x1, starting transfers between devices, spread(): lax.all_to_all(jnp.broadcast_to(part, (count,) + part.shape), axis, 0, 0)  19.6 us
    all_to_all x1, blocking collectives, on_device(): lax.all_to_all(row_lse.reshape(col_count, own_count), 'cols', 0, 0)  18.4 us
    all_to_all x1, waiting for transfers between devices, spread(): lax.all_to_all(jnp.broadcast_to(part, (count,) + part.shape), axis, 0, 0)  17.8 us
    unnamed x20, local copies, waits for them, and re-layouts  5.9 us
    reduce_max x1, other arithmetic, on_device(): col_top = jnp.max(col_score, axis=0)  2.83 us
    reduce_max x1, other arithmetic, on_device(): block_top = jnp.max(new_score, axis=1)  2.82 us
  transfers between devices with their start and end apart: 1, of which 1 were waited for; matrix products, arithmetic and copies ran while one was open for 1% of the time, Pallas kernels for 0%

profile of v1, /device:TPU:1, one launch (start us, length us, event | category | flops | bytes accessed | tf_op | source)
XLA Modules:
  0.0 137.9 jit_solution(4277246349194444458)
XLA Ops:
  0.6 0.0 copy-start
  0.6 0.0 copy-start.4
  0.7 0.7 copy-done
  1.3 0.1 broadcast_bitcast_fusion
  1.4 1.1 reshape.100
  2.5 19.6 %all-to-all-start = ((bf16[64,2,512]{2,1,0:T(2,128)(2,1)}), bf16[64,2,512]{2,1,0:T(2,128)(2,1)S(1)}, u32[]{:S(2)}, u32[]{:S(2)}) async-start(bf16[64,2,512]{2,1,0:T(2,128)(2,1)} %reshape.100), calls=%async_computation | async-start | bytes 262144 | tf_op jit(solution)/shard_map/all_to_all | solution.py:13
  22.1 0.8 multiply_reduce_fusion.1
  22.9 17.8 %all-to-all-done = bf16[64,2,512]{2,1,0:T(2,128)(2,1)S(1)} async-done(((bf16[64,2,512]{2,1,0:T(2,128)(2,1)}), bf16[64,2,512]{2,1,0:T(2,128)(2,1)S(1)}, u32[]{:S(2)}, u32[]{:S(2)}) %all-to-all-start) | async-done | bytes 131104 | tf_op jit(solution)/shard_map/all_to_all | solution.py:13
  40.7 0.3 reshape.101
  41.0 0.8 copy.45
  41.8 0.2 copy.47
  42.0 0.1 multiply_reduce_fusion
  42.1 0.5 reshape.88
  42.7 0.1 copy.46
  42.7 0.1 mul.61
  42.8 0.0 copy-done.4
  42.8 0.0 copy-done.6
  42.8 1.0 fusion
  43.8 0.0 copy-start.1
  43.8 1.9 %copy-done.1 = f32[2048,512]{0,1:T(8,128)} copy-done((f32[2048,512]{0,1:T(8,128)}, f32[2048,512]{0,1:T(8,128)S(1)}, u32[]{:S(2)}) %copy-start.1) | copy-done | bytes 4194328
  45.7 0.9 exponential_reduce_fusion.1
  46.7 0.1 add.50
  46.7 18.4 %all_to_all.39 = f32[64,1,32]{2,1,0:T(1,128)S(1)} all-to-all(f32[64,1,32]{2,1,0:T(1,128)S(1)} %bitcast.29), channel_id=1, replica_groups=mesh['rows'=8,'cols'=64] {'cols'}, dimensions={0} | all-to-all | bytes 16384 | tf_op jit(solution)/shard_map/all_to_all | solution.py:41
  65.1 0.1 reduce_max.55
  65.3 18.7 %all_to_all.40 = f32[64,1,32]{2,1,0:T(1,128)S(1)} all-to-all(f32[64,1,32]{2,1,0:T(1,128)S(1)} %broadcast_in_dim.11), channel_id=1, replica_groups=mesh['rows'=8,'cols'=64] {'cols'}, dimensions={0} | all-to-all | bytes 16384 | tf_op jit(solution)/shard_map/all_to_all | solution.py:13
  84.0 0.5 broadcast.62
  84.5 0.7 reduce.9
  85.2 0.1 sub.94
  85.3 2.8 %fusion.1 = f32[512]{0:T(512)S(1)} fusion(f32[2048,512]{0,1:T(8,128)} %copy-done.1, f32[2048]{0:T(1024)S(1)} %sub.94), kind=kLoop, calls=%fused_computation.9 | loop fusion | flops 3145216 | bytes 4204544 | tf_op jit(solution)/shard_map/reduce_max | solution.py:45
  88.1 0.6 copy-done.2
  88.7 0.9 exponential_reduce_fusion
  89.7 0.0 copy-done.7
  89.7 9.1 %all_to_all.41 = f32[8,1,512]{2,1,0:T(1,128)S(1)} all-to-all(f32[8,1,512]{2,1,0:T(1,128)S(1)} %broadcast_in_dim.12), channel_id=1, replica_groups=mesh['rows'=8,'cols'=64] {'rows'}, dimensions={0} | all-to-all | bytes 32768 | tf_op jit(solution)/shard_map/all_to_all | solution.py:13
  98.9 0.0 copy-start.5
  98.9 2.8 %fusion.2 = f32[2048]{0:T(1024)S(1)} fusion(f32[2048,512]{0,1:T(8,128)} %copy-done.1, f32[512]{0:T(512)S(1)} %add_multiply_fusion), kind=kLoop, calls=%fused_computation.10 | loop fusion | flops 3143680 | bytes 4204544 | tf_op jit(solution)/shard_map/reduce_max | solution.py:50
  101.7 0.6 copy-done.3
  102.3 1.1 convert_reduce_fusion
  103.4 0.5 fusion.7
  103.9 0.4 copy.50
  104.3 1.2 all_to_all.33
  105.5 30.4 %all_to_all.42 = f32[64,1,1088]{2,1,0:T(1,128)S(1)} all-to-all(f32[64,1,1088]{2,1,0:T(1,128)S(1)} %all_to_all.33), channel_id=1, replica_groups=mesh['rows'=8,'cols'=64] {'cols'}, dimensions={0} | all-to-all | bytes 557056 | tf_op jit(solution)/shard_map/all_to_all | solution.py:58
  135.9 0.2 copy.52
  136.2 0.3 slice_reduce_fusion.1
  136.5 0.1 subtract_exponential_fusion
  136.7 0.2 fusion.3
  136.9 0.2 slice_reduce_fusion
  137.1 0.1 fusion.4
  137.2 0.7 copy.53
  (18 shorter events, 0.3 us)
Async XLA Ops:
  0.6 0.7 copy-start
  0.6 42.2 %copy-start.4 = (bf16[32,512]{1,0:T(8,128)(2,1)S(1)}, bf16[32,512]{1,0:T(8,128)(2,1)}, u32[]{:S(2)}) copy-start(bf16[32,512]{1,0:T(8,128)(2,1)} %param.4) | copy-start | bytes 98308
  1.3 41.5 %copy-start.6 = (f32[512]{0:T(512)S(1)}, f32[512]{0:T(512)}, u32[]{:S(2)}) copy-start(f32[512]{0:T(512)} %param.5) | copy-start | bytes 6148
  2.5 38.2 %all-to-all-start = ((bf16[64,2,512]{2,1,0:T(2,128)(2,1)}), bf16[64,2,512]{2,1,0:T(2,128)(2,1)S(1)}, u32[]{:S(2)}, u32[]{:S(2)}) async-start(bf16[64,2,512]{2,1,0:T(2,128)(2,1)} %reshape.100), calls=%async_computation | async-start | bytes 262144 | tf_op jit(solution)/shard_map/all_to_all | solution.py:13
  43.8 1.9 %copy-start.1 = (f32[2048,512]{0,1:T(8,128)}, f32[2048,512]{0,1:T(8,128)S(1)}, u32[]{:S(2)}) copy-start(f32[2048,512]{0,1:T(8,128)S(1)} %get-tuple-element.24) | copy-start | bytes 12582916
  65.3 24.4 %copy-start.7 = (f32[32]{0:T(128)}, f32[32]{0:T(128)S(1)}, u32[]{:S(2)}) copy-start(f32[32]{0:T(128)S(1)} %add_multiply_fusion.1) | copy-start | bytes 388
  85.3 3.5 %copy-start.2 = (f32[2048,512]{0,1:T(8,128)S(1)}, f32[2048,512]{0,1:T(8,128)}, u32[]{:S(2)}) copy-start(f32[2048,512]{0,1:T(8,128)} %copy-done.1) | copy-start | bytes 12582916
  98.8 3.5 %copy-start.3 = (f32[2048,512]{0,1:T(8,128)S(1)}, f32[2048,512]{0,1:T(8,128)}, u32[]{:S(2)}) copy-start(f32[2048,512]{0,1:T(8,128)} %copy-done.1) | copy-start | bytes 12582916
  98.9 4.5 %copy-start.5 = (f32[512]{0:T(512)}, f32[512]{0:T(512)S(1)}, u32[]{:S(2)}) copy-start(f32[512]{0:T(512)S(1)} %add_multiply_fusion) | copy-start | bytes 6148

commit v2 on v1

v2 whole, which is shorter than its diff:
```python
import math

import jax
import jax.numpy as jnp
from jax import lax
from jax.experimental import pallas as pl
from jax.experimental.pallas import tpu as pltpu
from jax.sharding import Mesh, PartitionSpec as P

EPS = 0.25
SCALE = math.log2(math.e) / EPS
MARGIN = 18.0
AXES = ("x_lo", "y", "z", "x_hi", "core")
SHAPE = (2, 4, 16, 2, 2)
PLANE = ("x_lo", "y", "x_hi", "core")
BLOCK = 1024
LANES = 128
F32 = jnp.float32
BF16 = jnp.bfloat16


def row_index():
    return lax.axis_index("x_lo") * 4 + lax.axis_index("y")


def side_index():
    return lax.axis_index("x_hi") * 2 + lax.axis_index("core")


def lanes_of(shape):
    return lax.broadcasted_iota(jnp.int32, shape, len(shape) - 1)


def rows_of(shape):
    return lax.broadcasted_iota(jnp.int32, shape, len(shape) - 2)


def triple(value):
    high = value.astype(BF16).astype(F32)
    rest = value - high
    mid = rest.astype(BF16).astype(F32)
    return high, mid, rest - mid


def place(base, first, values):
    lane = lanes_of(base.shape)
    for step, value in enumerate(values):
        base = jnp.where(lane == first + step, value, base)
    return base


def turned(block):
    rows, cols = block.shape
    if rows < LANES:
        block = jnp.concatenate([block, jnp.zeros((LANES - rows, cols), block.dtype)], axis=0)
    return jnp.transpose(block)


def pair_up(block):
    half = block.shape[0] // 2
    return block[:half] + pltpu.roll(block[half:], 64, 1)


def split_up(packed, groups):
    wide = packed.astype(F32)
    rows = packed.shape[0] // groups
    low = wide.reshape(groups, 1, rows, LANES)
    high = pltpu.roll(wide, 64, 1).reshape(groups, 1, rows, LANES)
    both = jnp.concatenate([low, high], axis=1).reshape(groups * 2 * rows, LANES)
    return jnp.where(lanes_of(both.shape) < 64, both, 0.0)


def product(left, right):
    return lax.dot_general(left, right, (((1,), (1,)), ((), ())), preferred_element_type=F32)


def prepare(points_ref, samples_ref, potential_ref, points_out, samples_out):
    row = row_index()
    x = turned(points_ref[...].astype(F32))
    xp = jnp.concatenate([x, jnp.zeros((32, 96), F32)], axis=1) if x.shape[1] < LANES else x
    half_sq = -0.5 * jnp.sum(xp * xp, axis=1, keepdims=True)
    xp = place(xp, 32, (1.0, 1.0, 1.0) + triple(half_sq))
    points_out[...] = jnp.broadcast_to(pair_up(xp).astype(BF16)[None], (32, 16, LANES))
    start = pl.multiple_of(row // 2 * LANES, LANES)
    y = turned(samples_ref[:, pl.ds(start, LANES)].astype(F32))
    line = potential_ref[pl.ds(row // 2, 1), :]
    pot = jnp.transpose(jnp.broadcast_to(line, (LANES, LANES)))
    odd = row % 2 == 1
    y = jnp.where(odd, y[64:], y[:64])
    pot = jnp.where(odd, pot[64:], pot[:64])
    half_sq = -0.5 * jnp.sum(y * y, axis=1, keepdims=True)
    y = place(y, 32, triple(half_sq) + (1.0, 1.0, 1.0) + triple(pot) + (1.0, 1.0, 1.0))
    samples_out[...] = jnp.broadcast_to(pair_up(y).astype(BF16)[None], (16, 32, LANES))


def row_pass(points_ref, samples_ref, x_out, y_out, lse_out):
    x = split_up(points_ref[...], 32)
    packed = samples_ref[...].astype(F32)
    lane = lanes_of(packed.shape) % 64
    shift = jnp.max(jnp.where(lane == 38, packed, -1e30)) - MARGIN
    y = split_up(samples_ref[...], 16).astype(BF16)
    x_out[...] = x.astype(BF16)
    y_out[...] = y
    x = place(x, 38, (1.0, 1.0, 1.0) + triple(jnp.full((1, 1), -shift, F32))).astype(BF16)
    lse = jnp.zeros((8, LANES), F32)
    for tile in range(8):
        total = jnp.zeros((8, LANES), F32)
        for chunk in range(4):
            part = product(y[chunk * 256 : chunk * 256 + 256], x[tile * 128 : tile * 128 + 128])
            total += jnp.sum(jnp.exp2(part * SCALE).reshape(32, 8, LANES), axis=0)
        line = jnp.log2(jnp.sum(total, axis=0, keepdims=True)) + SCALE * shift
        lse = jnp.where(rows_of(lse.shape) == tile, line, lse)
    lse_out[...] = jnp.broadcast_to(lse[None], (32, 8, LANES))


def combine(lse):
    top = jnp.max(lse, axis=0)
    return top + jnp.log2(jnp.sum(jnp.exp2(lse - top[None]), axis=0))


def columns(block):
    flipped = turned(block)
    return jnp.concatenate(
        [jnp.broadcast_to(flipped[:, k : k + 1], (LANES, LANES)) for k in range(8)], axis=0
    )


def col_pass(x_ref, y_ref, rows_ref, lse_out, point_out, own_out):
    log_samples = math.log2(BLOCK * 32)
    point = log_samples - combine(rows_ref[...])
    point_out[...] = point
    me = row_index() * 4 + side_index()
    line = jnp.sum(jnp.where(rows_of(point.shape) == me // 4, point, 0.0), axis=0, keepdims=True)
    line = pltpu.roll(jnp.broadcast_to(line, (8, LANES)), (4 - me % 4) * 32 % LANES, 1)
    own_out[...] = line[:1, :32] / SCALE
    shift = jnp.max(point) - MARGIN * SCALE
    column = columns(point - shift)
    lse = jnp.zeros((8, LANES), F32)
    for tile in range(8):
        total = jnp.zeros((8, LANES), F32)
        y = y_ref[tile * 128 : tile * 128 + 128, :]
        for chunk in range(4):
            part = product(x_ref[chunk * 256 : chunk * 256 + 256, :], y)
            part = part * SCALE + column[chunk * 256 : chunk * 256 + 256]
            total += jnp.sum(jnp.exp2(part).reshape(32, 8, LANES), axis=0)
        line = jnp.log2(jnp.sum(total, axis=0, keepdims=True)) + shift
        lse = jnp.where(rows_of(lse.shape) == tile, line, lse)
    lse_out[...] = jnp.broadcast_to(lse[None], (16, 8, LANES))


def weigh(x_ref, y_ref, point_ref, cols_ref, parts_out):
    log_points = math.log2(BLOCK * 16)
    sample = log_points - combine(cols_ref[...])
    z = lax.axis_index("z")
    line = jnp.sum(jnp.where(rows_of(sample.shape) == z // 2, sample, 0.0), axis=0, keepdims=True)
    line = jnp.broadcast_to(line, (8, LANES)) / SCALE
    line = jnp.where(z % 2 == 1, line, pltpu.roll(line, 64, 1))
    column = columns(point_ref[...])
    y = y_ref[...]
    wide = jnp.where(lanes_of(y.shape) < 32, y.astype(F32), 0.0)
    wide = wide + pltpu.roll(wide, 32, 1)
    wide = wide + pltpu.roll(wide, 64, 1)
    right = jnp.concatenate([wide.astype(BF16), jnp.ones((BLOCK, LANES), BF16)], axis=1)
    lane = lanes_of((4, 8, LANES))
    for tile in range(8):
        x = x_ref[tile * 128 : tile * 128 + 128, :]
        total = jnp.zeros((LANES, 2 * LANES), F32)
        for chunk in range(4):
            rows = slice(chunk * 256, chunk * 256 + 256)
            part = product(x, y[rows]) * SCALE
            both = jnp.concatenate([sample[2 * chunk : 2 * chunk + 1], sample[2 * chunk + 1 : 2 * chunk + 2]], axis=1)
            one = column[tile * 128 : tile * 128 + 128]
            part = part + jnp.concatenate([one, one], axis=1) + both
            weight = jnp.exp2(part).astype(BF16)
            total += jnp.dot(weight, right[rows], preferred_element_type=F32)
        numer = total[:, :LANES].reshape(4, 4, 8, LANES)
        denom = total[:, LANES:].reshape(4, 4, 8, LANES)
        first = numer[:, 0]
        second = denom[:, 0]
        for q in range(1, 4):
            first = jnp.where(lane // 32 == q, numer[:, q], first)
            second = jnp.where(lane // 16 == q, denom[:, q], second)
        second = jnp.where(lane >= 64, line[None], second)
        parts_out[tile * 4 : tile * 4 + 4, :8, :] = first
        parts_out[tile * 4 : tile * 4 + 4, 8:, :] = second


def finish(parts_ref, bary_out, sample_out):
    total = jnp.sum(parts_ref[...], axis=0)
    numer, denom = total[:8], total[8:]
    lane = lanes_of((8, LANES))
    below = jnp.broadcast_to(denom[:, :1], (8, LANES))
    for q in range(1, 4):
        below = jnp.where(lane // 32 == q, jnp.broadcast_to(denom[:, 16 * q : 16 * q + 1], (8, LANES)), below)
    ratio = numer / below
    stack = jnp.concatenate([ratio] + [pltpu.roll(ratio, LANES - 32 * q, 1) for q in range(1, 4)], axis=0)
    bary_out[...] = turned(stack)[:32, :32]
    side = side_index()
    lines = []
    for pair in range(4):
        even = parts_ref[pl.ds(8 * pair + side, 1), 8:, :][0]
        odd = parts_ref[pl.ds(8 * pair + 4 + side, 1), 8:, :][0]
        lines.append(jnp.where(lane < 64, pltpu.roll(even, 64, 1), odd)[:1])
    sample_out[...] = jnp.concatenate(lines, axis=0)


def call(body, outs, *args):
    vmem = pl.BlockSpec(memory_space=pltpu.VMEM)
    return pl.pallas_call(
        body,
        out_shape=[jax.ShapeDtypeStruct(shape, dtype) for shape, dtype in outs],
        in_specs=[vmem] * len(args),
        out_specs=[vmem] * len(outs),
    )(*args)


def on_device(points, samples, potential):
    xs, ys = call(
        prepare,
        [((32, 16, LANES), BF16), ((16, 32, LANES), BF16)],
        points, samples, potential.reshape(4, LANES),
    )
    xs = lax.all_to_all(xs, PLANE, 0, 0).reshape(512, LANES)
    ys = lax.all_to_all(ys, "z", 0, 0).reshape(512, LANES)
    x, y, rows = call(
        row_pass,
        [((BLOCK, LANES), BF16), ((BLOCK, LANES), BF16), ((32, 8, LANES), F32)],
        xs, ys,
    )
    rows = lax.all_to_all(rows, PLANE, 0, 0)
    cols, point, own = call(
        col_pass,
        [((16, 8, LANES), F32), ((8, LANES), F32), ((1, 32), F32)],
        x, y, rows,
    )
    cols = lax.all_to_all(cols, "z", 0, 0)
    (parts,) = call(weigh, [((32, 16, LANES), F32)], x, y, point, cols)
    parts = lax.all_to_all(parts, PLANE, 0, 0)
    bary, sample = call(finish, [((32, 32), F32), ((4, LANES), F32)], parts)
    return own.reshape(32), sample.reshape(512), bary


def solution(mesh):
    split = Mesh(mesh.devices.reshape(SHAPE), AXES)
    return jax.shard_map(
        on_device,
        mesh=split,
        in_specs=(P(None, AXES), P(None, ("z", "x_hi", "core")), P(("z", "x_hi", "core"))),
        out_specs=(P(AXES), P(("z", "x_hi", "core")), P(None, AXES)),
        check_vma=False,
    )
```

time: 138 us -> 103 us (0.75)
  starting transfers between devices: 19.6 us -> 0 us
  waiting for transfers between devices: 17.8 us -> 0 us
  blocking collectives: 76.6 us -> 89.1 us
  Pallas kernels: 0 us -> 12.3 us
  other arithmetic: 11.2 us -> 0 us
  local copies, waits for them, and re-layouts: 10.3 us -> 0.01 us
  matrix products: 1.44 us -> 0 us
    all_to_all x1 -> x0, starting transfers between devices: 19.6 us -> none  [spread(): lax.all_to_all(jnp.broadcast_to(part, (count,) + part.shape), axis, 0, 0)]
    all_to_all x1 -> x0, waiting for transfers between devices: 17.8 us -> none  [spread(): lax.all_to_all(jnp.broadcast_to(part, (count,) + part.shape), axis, 0, 0)]
    all_to_all x4 -> x5, blocking collectives: 76.6 us -> 89.1 us  [the longest x1 24.4 us: on_device(): ys = lax.all_to_all(ys, 'z', 0, 0).reshape(512, LANES)]
    pallas_call x0 -> x5, Pallas kernels: none -> 12.3 us  [call(): pl.pallas_call(body, out_shape=[jax.ShapeDtypeStruct(shape, dtype) for sh...]
    reduce_max x5 -> x0, other arithmetic: 6.09 us -> none  [the longest x1 2.83 us: on_device(): col_top = jnp.max(col_score, axis=0)]
    unnamed x20 -> x2, local copies, waits for them, and re-layouts: 5.9 us -> 0.01 us
    reduce_sum x8 -> x0, other arithmetic: 4.12 us -> none  [the longest x1 1.08 us: on_device(): denom = jnp.sum(weight.astype(jnp.float32), axis=1)]
    all_to_all x5 -> x0, local copies, waits for them, and re-layouts: 2.98 us -> none  [the longest x3 1.5 us: spread(): lax.all_to_all(jnp.broadcast_to(part, (count,) + part.shape), axis, 0, 0)]
  transfers between devices with their start and end apart: 1 -> 0, of which waited for: 1 -> 0; matrix products, arithmetic and copies ran while one was open for 1% -> 0% of each run, Pallas kernels for 0% -> 0%
where the time goes in v2:
time: 103 us; the launch traced here: 102 us
  blocking collectives  89.1 us (87%)
  Pallas kernels  12.3 us (12%)
    all_to_all x1, blocking collectives, on_device(): ys = lax.all_to_all(ys, 'z', 0, 0).reshape(512, LANES)  24.4 us
    all_to_all x1, blocking collectives, on_device(): xs = lax.all_to_all(xs, PLANE, 0, 0).reshape(512, LANES)  18.7 us
    all_to_all x1, blocking collectives, on_device(): cols = lax.all_to_all(cols, 'z', 0, 0)  15.8 us
    all_to_all x1, blocking collectives, on_device(): rows = lax.all_to_all(rows, PLANE, 0, 0)  15.1 us
    all_to_all x1, blocking collectives, on_device(): parts = lax.all_to_all(parts, PLANE, 0, 0)  15 us
    pallas_call x5, Pallas kernels, call(): pl.pallas_call(body, out_shape=[jax.ShapeDtypeStruct(shape, dtype) for sh...  12.3 us

profile of v2, /device:TPU:1, one launch (start us, length us, event | category | flops | bytes accessed | tf_op | source)
XLA Modules:
  0.0 102.0 jit_solution(6357424422802932262)
XLA Ops:
  0.6 1.7 %shard_map.58 = (bf16[32,16,128]{2,1,0:T(8,128)(2,1)}, bf16[16,32,128]{2,1,0:T(8,128)(2,1)}) custom-call(bf16[32,32]{1,0:T(8,128)(2,1)} %points_ref.1, bf16[32,512]{1,0:T(8,128)(2,1)} %samples_ref.1, f32[4,128]{1,0:T(4,128)} %bitcast.7), custom_call_target="tpu_custom_call" | custom-call | tf_op jit(solution)/shard_map/pallas_call | solution.py:209
  2.4 0.0 copy-start
  2.4 18.7 %all_to_all.25 = bf16[32,16,128]{2,1,0:T(8,128)(2,1)} all-to-all(bf16[32,16,128]{2,1,0:T(8,128)(2,1)} %get-tuple-element.13), channel_id=1, replica_groups=mesh['x_lo'=2,'y'=4,'z'=16,'x_hi'=2,'core'=2] {'x_lo','y','x_hi','core'}, dimensions={0} | all-to-all | bytes 262144 | tf_op jit(solution)/shard_map/all_to_all | solution.py:223
  21.1 0.0 copy-done
  21.1 24.4 %all_to_all.26 = bf16[16,32,128]{2,1,0:T(8,128)(2,1)} all-to-all(bf16[16,32,128]{2,1,0:T(8,128)(2,1)S(1)} %copy-done), channel_id=1, replica_groups=mesh['x_lo'=2,'y'=4,'z'=16,'x_hi'=2,'core'=2] {'z'}, dimensions={0} | all-to-all | bytes 262144 | tf_op jit(solution)/shard_map/all_to_all | solution.py:224
  45.5 2.6 %shard_map.59 = (bf16[1024,128]{1,0:T(8,128)(2,1)}, bf16[1024,128]{1,0:T(8,128)(2,1)}, f32[32,8,128]{2,1,0:T(8,128)}) custom-call(bf16[512,128]{1,0:T(8,128)(2,1)} %bitcast.5, bf16[512,128]{1,0:T(8,128)(2,1)} %bitcast.6), custom_call_target="tpu_custom_call" | custom-call | tf_op jit(solution)/shard_map/pallas_call | solution.py:209
  48.1 15.1 %all_to_all.27.rows_ref = f32[32,8,128]{2,1,0:T(8,128)} all-to-all(f32[32,8,128]{2,1,0:T(8,128)} %get-tuple-element.17), channel_id=1, replica_groups=mesh['x_lo'=2,'y'=4,'z'=16,'x_hi'=2,'core'=2] {'x_lo','y','x_hi','core'}, dimensions={0} | all-to-all | bytes 262144 | tf_op jit(solution)/shard_map/all_to_all | solution.py:230
  63.2 2.8 %shard_map.60 = (f32[16,8,128]{2,1,0:T(8,128)}, f32[8,128]{1,0:T(8,128)}, f32[1,32]{1,0:T(1,128)}) custom-call(bf16[1024,128]{1,0:T(8,128)(2,1)} %get-tuple-element.15.x_ref, bf16[1024,128]{1,0:T(8,128)(2,1)} %get-tuple-element.16.y_ref, f32[32,8,128]{2,1,0:T(8,128)} %all_to_all.27.rows_ref), custom_call_target="tpu_custom_call" | custom-call | tf_op jit(solution)/shard_map/pallas_call | solution.py:209
  66.0 15.8 %all_to_all.28.cols_ref = f32[16,8,128]{2,1,0:T(8,128)} all-to-all(f32[16,8,128]{2,1,0:T(8,128)} %get-tuple-element.20), channel_id=1, replica_groups=mesh['x_lo'=2,'y'=4,'z'=16,'x_hi'=2,'core'=2] {'z'}, dimensions={0} | all-to-all | bytes 131072 | tf_op jit(solution)/shard_map/all_to_all | solution.py:236
  81.8 3.3 %shard_map.61 = f32[32,16,128]{2,1,0:T(8,128)} custom-call(bf16[1024,128]{1,0:T(8,128)(2,1)} %get-tuple-element.15.x_ref, bf16[1024,128]{1,0:T(8,128)(2,1)} %get-tuple-element.16.y_ref, f32[8,128]{1,0:T(8,128)} %get-tuple-element.19.point_ref, f32[16,8,128]{2,1,0:T(8,128)} %all_to_all.28.cols_ref), custom_call_target="tpu_custom_call" | custom-call | tf_op jit(solution)/shard_map/pallas_call | solution.py:209
  85.2 15.0 %all_to_all.29.parts_ref = f32[32,16,128]{2,1,0:T(8,128)} all-to-all(f32[32,16,128]{2,1,0:T(8,128)} %shard_map.61), channel_id=1, replica_groups=mesh['x_lo'=2,'y'=4,'z'=16,'x_hi'=2,'core'=2] {'x_lo','y','x_hi','core'}, dimensions={0} | all-to-all | bytes 524288 | tf_op jit(solution)/shard_map/all_to_all | solution.py:238
  100.2 1.8 %shard_map.62 = (f32[32,32]{1,0:T(8,128)}, f32[4,128]{1,0:T(4,128)}) custom-call(f32[32,16,128]{2,1,0:T(8,128)} %all_to_all.29.parts_ref), custom_call_target="tpu_custom_call" | custom-call | tf_op jit(solution)/shard_map/pallas_call | solution.py:209
Async XLA Ops:
  2.4 18.7 %copy-start = (bf16[16,32,128]{2,1,0:T(8,128)(2,1)S(1)}, bf16[16,32,128]{2,1,0:T(8,128)(2,1)}, u32[]{:S(2)}) copy-start(bf16[16,32,128]{2,1,0:T(8,128)(2,1)} %get-tuple-element.14) | copy-start | bytes 393220

commit v3 on v1

v3 whole, which is shorter than its diff:
```python
import math

import jax
import jax.numpy as jnp
from jax import lax
from jax.experimental import pallas as pl
from jax.experimental.pallas import tpu as pltpu
from jax.sharding import Mesh, PartitionSpec as P

EPS = 0.25
SCALE = math.log2(math.e) / EPS
MARGIN = 18.0
AXES = ("x_lo", "y", "z", "x_hi", "core")
SHAPE = (2, 4, 16, 2, 2)
PLANE = ("x_lo", "y", "x_hi", "core")
POINTS = 512
SAMPLES = 2048
LOG_POINTS = math.log2(POINTS * 32)
LOG_SAMPLES = math.log2(SAMPLES * 16)
LANES = 128
DEPTH = 48
F32 = jnp.float32
BF16 = jnp.bfloat16


def lanes_of(shape):
    return lax.broadcasted_iota(jnp.int32, shape, len(shape) - 1)


def rows_of(shape):
    return lax.broadcasted_iota(jnp.int32, shape, len(shape) - 2)


def triple(value):
    high = value.astype(BF16).astype(F32)
    rest = value - high
    mid = rest.astype(BF16).astype(F32)
    return high, mid, rest - mid


def turned(block):
    rows, cols = block.shape
    if rows < LANES:
        block = jnp.concatenate([block, jnp.zeros((LANES - rows, cols), block.dtype)], axis=0)
    return jnp.transpose(block)


def combine(lse):
    top = jnp.max(lse, axis=0)
    return top + jnp.log2(jnp.sum(jnp.exp2(lse - top[None]), axis=0))


def line_up(block):
    return jnp.concatenate([block[k : k + 1] for k in range(block.shape[0])], axis=1)


def stack_up(lines):
    lane = rows_of((len(lines), LANES))
    block = jnp.broadcast_to(lines[0], lane.shape)
    for k, line in enumerate(lines[1:], 1):
        block = jnp.where(lane == k, line, block)
    return block


def extra_rows(value):
    row = rows_of((16, value.shape[1]))
    block = jnp.where((row >= 3) & (row < 9), 1.0, 0.0)
    for k, part in enumerate(triple(value)):
        block = jnp.where(row == k, part, block)
    return block.astype(BF16)


def prepare_points(points_ref, points_out):
    x = turned(points_ref[...].astype(F32))
    packed = x[:8]
    for q in range(1, 4):
        packed = packed + pltpu.roll(x[8 * q : 8 * q + 8], 32 * q, 1)
    points_out[...] = jnp.broadcast_to(packed.astype(BF16)[None], (16, 8, LANES))


def prepare_samples(samples_ref, potential_ref, samples_out):
    samples_out[:32, :] = samples_ref[...]
    pot = potential_ref[...]
    row = rows_of((8, 512))
    block = jnp.zeros((8, 512), F32)
    for k, part in enumerate(triple(pot)):
        block = jnp.where(row == k, part, block)
    samples_out[32:, :] = block.astype(BF16)


def row_pass(points_ref, own_ref, core_ref, side_ref, both_ref, x_out, y_out, lse_out):
    packed = points_ref[...].astype(F32)
    x = jnp.concatenate(
        [packed.reshape(16, 1, 8, LANES)]
        + [pltpu.roll(packed, LANES - 32 * q, 1).reshape(16, 1, 8, LANES) for q in range(1, 4)],
        axis=1,
    ).reshape(POINTS, LANES)
    lane = lanes_of(x.shape)
    x = jnp.where(lane < 32, x, 0.0)
    x_norm = -0.5 * jnp.sum(x * x, axis=1, keepdims=True)
    x = jnp.where((lane >= 32) & (lane < 35), 1.0, x)
    for k, part in enumerate(triple(x_norm)):
        x = jnp.where(lane == 35 + k, part, x)
    x = x[:, :DEPTH].astype(BF16)
    x_out[...] = x
    side = lax.axis_index("x_hi") == 1
    core = lax.axis_index("core") == 1
    blocks = [ref[...].astype(F32) for ref in (own_ref, core_ref, side_ref, both_ref)]
    swap = [blocks[1], blocks[0], blocks[3], blocks[2]]
    blocks = [jnp.where(core, b, a) for a, b in zip(blocks, swap)]
    swap = blocks[2:] + blocks[:2]
    y = jnp.concatenate([jnp.where(side, b, a) for a, b in zip(blocks, swap)], axis=1)
    pot = jnp.sum(y[32:40], axis=0, keepdims=True)
    y = y[:32]
    y_norm = -0.5 * jnp.sum(y * y, axis=0, keepdims=True)
    shift = jnp.max(pot) - MARGIN
    y_out[:32, :] = y.astype(BF16)
    y_out[32:, :] = extra_rows(y_norm)
    y = jnp.concatenate([y.astype(BF16), extra_rows(y_norm + pot - shift)], axis=0)
    lines = []
    for tile in range(4):
        total = jnp.zeros((LANES, LANES), F32)
        left = x[tile * 128 : tile * 128 + 128]
        for chunk in range(8):
            right = y[:, chunk * 256 : chunk * 256 + 256]
            part = jnp.exp2(jnp.dot(left, right, preferred_element_type=F32) * SCALE)
            total += part[:, :LANES] + part[:, LANES:]
        total = jnp.sum(jnp.transpose(total), axis=0, keepdims=True)
        lines.append(jnp.log2(total) + SCALE * shift)
    lse_out[...] = jnp.broadcast_to(stack_up(lines)[None], (16, 4, LANES))


def col_pass(x_ref, y_ref, rows_ref, x_out, shift_out, lse_out, own_out):
    point = (LOG_SAMPLES - combine(rows_ref[...])) / SCALE
    z = lax.axis_index("z")
    line = jnp.sum(jnp.where(rows_of(point.shape) == z // 4, point, 0.0), axis=0, keepdims=True)
    line = pltpu.roll(jnp.broadcast_to(line, (8, LANES)), (4 - z % 4) * 32 % LANES, 1)
    own_out[...] = line[:1, :32]
    shift = jnp.max(point) - MARGIN
    shift_out[...] = jnp.full((1, LANES), shift, F32)
    flipped = turned(point - shift)
    x = x_ref[...].astype(F32)
    column = jnp.concatenate([flipped[:, k : k + 1] for k in range(4)], axis=0)
    lane = lanes_of(x.shape)
    for k, part in enumerate(triple(column)):
        x = jnp.where(lane == 38 + k, part, x)
    x = x.astype(BF16)
    x_out[...] = x
    lines = []
    for chunk in range(8):
        total = jnp.zeros((8, 256), F32)
        right = y_ref[:, chunk * 256 : chunk * 256 + 256]
        for tile in range(4):
            left = x[tile * 128 : tile * 128 + 128]
            part = jnp.exp2(jnp.dot(left, right, preferred_element_type=F32) * SCALE)
            total += jnp.sum(part.reshape(16, 8, 256), axis=0)
        total = jnp.log2(jnp.sum(total, axis=0, keepdims=True)) + SCALE * shift
        lines += [total[:, :LANES], total[:, LANES:]]
    lse_out[...] = jnp.broadcast_to(stack_up(lines)[None], (32, 16, LANES))


def weigh(x_ref, y_ref, shift_ref, cols_ref, parts_out, sample_out):
    sample = (LOG_POINTS - combine(cols_ref[...])) / SCALE
    side = lax.axis_index("x_hi") * 2 + lax.axis_index("core")
    own = sample[:4]
    for k in range(1, 4):
        own = jnp.where(side == k, sample[4 * k : 4 * k + 4], own)
    sample_out[...] = own
    y = y_ref[:32, :]
    y_norm = jnp.sum(y_ref[32:, :].astype(F32)[:3], axis=0, keepdims=True)
    shift = jnp.max(shift_ref[...])
    y_all = jnp.concatenate([y, extra_rows(y_norm + line_up(sample) + shift)], axis=0)
    right = jnp.concatenate([y, y, y, y, jnp.ones((LANES, SAMPLES), BF16)], axis=0)
    lane = lanes_of((4, 8, LANES))
    for tile in range(4):
        x = x_ref[tile * 128 : tile * 128 + 128, :]
        total = jnp.zeros((LANES, 2 * LANES), F32)
        for chunk in range(8):
            cols = slice(chunk * 256, chunk * 256 + 256)
            weight = jnp.exp2(jnp.dot(x, y_all[:, cols], preferred_element_type=F32) * SCALE)
            total += lax.dot_general(
                weight.astype(BF16),
                right[:, cols],
                (((1,), (1,)), ((), ())),
                preferred_element_type=F32,
            )
        numer = total[:, :LANES].reshape(4, 4, 8, LANES)
        denom = total[:, LANES:].reshape(4, 4, 8, LANES)
        first, second = numer[:, 0], denom[:, 0]
        for q in range(1, 4):
            first = jnp.where(lane // 32 == q, numer[:, q], first)
            second = jnp.where(lane // 32 == q, denom[:, q], second)
        parts_out[tile * 4 : tile * 4 + 4, :8, :] = first
        parts_out[tile * 4 : tile * 4 + 4, 8:, :] = second


def finish(parts_ref, bary_out):
    total = jnp.sum(parts_ref[...], axis=0)
    ratio = total[:8] / total[8:]
    stack = jnp.concatenate([ratio] + [pltpu.roll(ratio, LANES - 32 * q, 1) for q in range(1, 4)], axis=0)
    bary_out[...] = turned(stack)[:32, :32]


def call(body, outs, *args):
    vmem = pl.BlockSpec(memory_space=pltpu.VMEM)
    return pl.pallas_call(
        body,
        out_shape=[jax.ShapeDtypeStruct(shape, dtype) for shape, dtype in outs],
        in_specs=[vmem] * len(args),
        out_specs=[vmem] * len(outs),
        compiler_params=pltpu.CompilerParams(vmem_limit_bytes=8 << 20),
    )(*args)


def on_device(points, samples, potential):
    (xs,) = call(prepare_points, [((16, 8, LANES), BF16)], points)
    xs = lax.all_to_all(xs, "z", 0, 0).reshape(LANES, LANES)
    (own,) = call(prepare_samples, [((40, 512), BF16)], samples, potential.reshape(1, 512))
    core = lax.ppermute(own, "core", [(0, 1), (1, 0)])
    side = lax.ppermute(own, "x_hi", [(0, 1), (1, 0)])
    both = lax.ppermute(own, ("x_hi", "core"), [(k, 3 - k) for k in range(4)])
    x, y, rows = call(
        row_pass,
        [((POINTS, DEPTH), BF16), ((DEPTH, SAMPLES), BF16), ((16, 4, LANES), F32)],
        xs, own, core, side, both,
    )
    rows = lax.all_to_all(rows, "z", 0, 0)
    x, shift, cols, point = call(
        col_pass,
        [((POINTS, DEPTH), BF16), ((1, LANES), F32), ((32, 16, LANES), F32), ((1, 32), F32)],
        x, y, rows,
    )
    cols = lax.all_to_all(cols, PLANE, 0, 0)
    parts, sample = call(
        weigh, [((16, 16, LANES), F32), ((4, LANES), F32)], x, y, shift, cols
    )
    parts = lax.all_to_all(parts, "z", 0, 0)
    (bary,) = call(finish, [((32, 32), F32)], parts)
    return point.reshape(32), sample.reshape(512), bary


def solution(mesh):
    split = Mesh(mesh.devices.reshape(SHAPE), AXES)
    cols = ("z", "x_hi", "core")
    return jax.shard_map(
        on_device,
        mesh=split,
        in_specs=(P(None, AXES), P(None, cols), P(cols)),
        out_specs=(P(AXES), P(cols), P(None, AXES)),
        check_vma=False,
    )
```

time: 138 us -> 91.5 us (0.66); the launches traced: 138 us -> 89.8 us
  blocking collectives: 76.6 us -> 53.1 us
  waiting for transfers between devices: 17.8 us -> 2.73 us
  other arithmetic: 11.2 us -> 0 us
  local copies, waits for them, and re-layouts: 10.3 us -> 0.7 us
  Pallas kernels: 0 us -> 6.95 us
  starting transfers between devices: 19.6 us -> 25.6 us
  matrix products: 1.44 us -> 0 us
    all_to_all x4 -> x3, blocking collectives: 76.6 us -> 53.1 us  [the longest x1 22.5 us: on_device(): rows = lax.all_to_all(rows, 'z', 0, 0)]
    all_to_all x1, waiting for transfers between devices: 17.8 us -> 0.01 us  [on_device(): xs = lax.all_to_all(xs, 'z', 0, 0).reshape(LANES, LANES)]
    ppermute x0 -> x3, starting transfers between devices: none -> 9.72 us  [the longest x1 5.49 us: on_device(): both = lax.ppermute(own, ('x_hi', 'core'), [(k, 3 - k) for k in range(4)])]
    pallas_call x0 -> x6, Pallas kernels: none -> 6.95 us  [call(): pl.pallas_call(body, out_shape=[jax.ShapeDtypeStruct(shape, dtype) for sh...]
    reduce_max x5 -> x0, other arithmetic: 6.09 us -> none  [the longest x1 2.83 us: on_device(): col_top = jnp.max(col_score, axis=0)]
    unnamed x20 -> x6, local copies, waits for them, and re-layouts: 5.9 us -> 0.7 us
    reduce_sum x8 -> x0, other arithmetic: 4.12 us -> none  [the longest x1 1.08 us: on_device(): denom = jnp.sum(weight.astype(jnp.float32), axis=1)]
    all_to_all x1, starting transfers between devices: 19.6 us -> 15.9 us  [on_device(): xs = lax.all_to_all(xs, 'z', 0, 0).reshape(LANES, LANES)]
  transfers between devices with their start and end apart: 1 -> 4, of which waited for: 1 -> 1; matrix products, arithmetic and copies ran while one was open for 1% -> 0% of each run, Pallas kernels for 0% -> 0%
where the time goes in v3:
time: 91.5 us; the launch traced here: 89.8 us
  blocking collectives  53.1 us (58%)
  starting transfers between devices  25.6 us (28%)
  Pallas kernels  6.95 us (8%)
  waiting for transfers between devices  2.73 us (3%)
    all_to_all x1, blocking collectives, on_device(): rows = lax.all_to_all(rows, 'z', 0, 0)  22.5 us
    all_to_all x1, blocking collectives, on_device(): cols = lax.all_to_all(cols, PLANE, 0, 0)  16 us
    all_to_all x1, starting transfers between devices, on_device(): xs = lax.all_to_all(xs, 'z', 0, 0).reshape(LANES, LANES)  15.9 us
    all_to_all x1, blocking collectives, on_device(): parts = lax.all_to_all(parts, 'z', 0, 0)  14.6 us
    pallas_call x6, Pallas kernels, call(): pl.pallas_call(body, out_shape=[jax.ShapeDtypeStruct(shape, dtype) for sh...  6.95 us
    ppermute x1, starting transfers between devices, on_device(): both = lax.ppermute(own, ('x_hi', 'core'), [(k, 3 - k) for k in range(4)])  5.49 us
    ppermute x1, waiting for transfers between devices, on_device(): side = lax.ppermute(own, 'x_hi', [(0, 1), (1, 0)])  2.72 us
    ppermute x1, starting transfers between devices, on_device(): side = lax.ppermute(own, 'x_hi', [(0, 1), (1, 0)])  2.13 us
  transfers between devices with their start and end apart: 4, of which 1 were waited for; matrix products, arithmetic and copies ran while one was open for 0% of the time, Pallas kernels for 0%

profile of v3, /device:TPU:1, one launch (start us, length us, event | category | flops | bytes accessed | tf_op | source)
XLA Modules:
  0.0 89.8 jit_solution(17212237033602623956)
XLA Ops:
  0.6 0.0 copy-start.1
  0.6 0.7 copy-done.1
  1.3 0.8 shard_map.58
  2.1 0.0 copy-start
  2.1 0.0 copy-start.2
  2.1 15.9 %all-to-all-start = ((bf16[16,8,128]{2,1,0:T(8,128)(2,1)}), bf16[16,8,128]{2,1,0:T(8,128)(2,1)S(1)}, u32[]{:S(2)}, u32[]{:S(2)}) async-start(bf16[16,8,128]{2,1,0:T(8,128)(2,1)} %shard_map.58), calls=%async_computation | async-start | bytes 65536 | tf_op jit(solution)/shard_map/all_to_all | solution.py:217
  18.0 0.0 copy-done
  18.0 0.0 copy-done.2
  18.0 5.5 %collective-permute-start.2 = (bf16[40,512]{1,0:T(8,128)(2,1)S(1)}, bf16[40,512]{1,0:T(8,128)(2,1)S(1)}, u32[]{:S(2)}, u32[]{:S(2)}) collective-permute-start(bf16[40,512]{1,0:T(8,128)(2,1)S(1)} %shard_map.59.own_ref), channel_id=1, source_target_pairs={{0,3},{1,2},{2,1},{3,0},{4,7},{5,6},{6,5},{7,4},{8,11},{9,10},{10,... | collective-permute-start | bytes 122888 | tf_op jit(solution)/shard_map/ppermute | solution.py:221
  23.5 2.1 %collective-permute-start.1 = (bf16[40,512]{1,0:T(8,128)(2,1)S(1)}, bf16[40,512]{1,0:T(8,128)(2,1)S(1)}, u32[]{:S(2)}, u32[]{:S(2)}) collective-permute-start(bf16[40,512]{1,0:T(8,128)(2,1)S(1)} %shard_map.59.own_ref), channel_id=1, source_target_pairs={{0,2},{2,0},{1,3},{3,1},{4,6},{6,4},{5,7},{7,5},{8,10},{10,8},{9,1... | collective-permute-start | bytes 122888 | tf_op jit(solution)/shard_map/ppermute | solution.py:220
  25.7 2.1 %collective-permute-start = (bf16[40,512]{1,0:T(8,128)(2,1)S(1)}, bf16[40,512]{1,0:T(8,128)(2,1)S(1)}, u32[]{:S(2)}, u32[]{:S(2)}) collective-permute-start(bf16[40,512]{1,0:T(8,128)(2,1)S(1)} %shard_map.59.own_ref), channel_id=1, source_target_pairs={{0,1},{1,0},{2,3},{3,2},{4,5},{5,4},{6,7},{7,6},{8,9},{9,8},{10,11... | collective-permute-start | bytes 122888 | tf_op jit(solution)/shard_map/ppermute | solution.py:219
  27.8 0.0 collective-permute-done.2.both_ref
  27.8 2.7 %collective-permute-done.1.side_ref = bf16[40,512]{1,0:T(8,128)(2,1)S(1)} collective-permute-done((bf16[40,512]{1,0:T(8,128)(2,1)S(1)}, bf16[40,512]{1,0:T(8,128)(2,1)S(1)}, u32[]{:S(2)}, u32[]{:S(2)}) %collective-permute-start.1) | collective-permute-done | bytes 40992 | tf_op jit(solution)/shard_map/ppermute | solution.py:220
  30.5 0.0 collective-permute-done.core_ref
  30.5 0.0 all-to-all-done
  30.5 1.0 %shard_map.60 = (bf16[512,48]{1,0:T(8,128)(2,1)S(1)}, bf16[48,2048]{1,0:T(8,128)(2,1)S(1)}, f32[16,4,128]{2,1,0:T(4,128)S(1)}) custom-call(bf16[128,128]{1,0:T(8,128)(2,1)S(1)} %bitcast.4, bf16[40,512]{1,0:T(8,128)(2,1)S(1)} %shard_map.59.own_ref, bf16[40,512]{1,0:T(8,128)(2,1)S(1)} %collective-permute-done.core_ref, ...), custom_call_target="tpu_custom_call" | custom-call | tf_op jit(solution)/shard_map/pallas_call | solution.py:206
  31.5 22.5 %all_to_all.20.rows_ref = f32[16,4,128]{2,1,0:T(4,128)S(1)} all-to-all(f32[16,4,128]{2,1,0:T(4,128)S(1)} %get-tuple-element.14), channel_id=1, replica_groups=mesh['x_lo'=2,'y'=4,'z'=16,'x_hi'=2,'core'=2] {'z'}, dimensions={0} | all-to-all | bytes 65536 | tf_op jit(solution)/shard_map/all_to_all | solution.py:227
  54.0 1.6 %shard_map.61 = (bf16[512,48]{1,0:T(8,128)(2,1)S(1)}, f32[1,128]{1,0:T(1,128)S(1)}, f32[32,16,128]{2,1,0:T(8,128)S(1)}, f32[1,32]{1,0:T(1,128)}) custom-call(bf16[512,48]{1,0:T(8,128)(2,1)S(1)} %get-tuple-element.12.x_ref, bf16[48,2048]{1,0:T(8,128)(2,1)S(1)} %get-tuple-element.13.y_ref, f32[16,4,128]{2,1,0:T(4,128)S(1)} %all_to_all.20.rows_ref), custom_call_target="tpu_custom_call" | custom-call | tf_op jit(solution)/shard_map/pallas_call | solution.py:206
  55.6 16.0 %all_to_all.21.cols_ref = f32[32,16,128]{2,1,0:T(8,128)S(1)} all-to-all(f32[32,16,128]{2,1,0:T(8,128)S(1)} %get-tuple-element.18), channel_id=1, replica_groups=mesh['x_lo'=2,'y'=4,'z'=16,'x_hi'=2,'core'=2] {'x_lo','y','x_hi','core'}, dimensions={0} | all-to-all | bytes 524288 | tf_op jit(solution)/shard_map/all_to_all | solution.py:233
  71.6 2.8 %shard_map.62 = (f32[16,16,128]{2,1,0:T(8,128)S(1)}, f32[4,128]{1,0:T(4,128)}) custom-call(bf16[512,48]{1,0:T(8,128)(2,1)S(1)} %get-tuple-element.16.x_ref, bf16[48,2048]{1,0:T(8,128)(2,1)S(1)} %get-tuple-element.13.y_ref, f32[1,128]{1,0:T(1,128)S(1)} %get-tuple-element.17.shift_ref, f32[32,16,128]{2,1,0:T(8,128)S(1)} %all_to_all.21.cols_ref), custom_call_target="tpu_custom_call" | custom-call | tf_op jit(solution)/shard_map/pallas_call | solution.py:206
  74.4 14.6 %all_to_all.22.parts_ref = f32[16,16,128]{2,1,0:T(8,128)S(1)} all-to-all(f32[16,16,128]{2,1,0:T(8,128)S(1)} %get-tuple-element.20), channel_id=1, replica_groups=mesh['x_lo'=2,'y'=4,'z'=16,'x_hi'=2,'core'=2] {'z'}, dimensions={0} | all-to-all | bytes 262144 | tf_op jit(solution)/shard_map/all_to_all | solution.py:237
  89.0 0.8 shard_map.63
  (1 shorter events, 0.0 us)
Async XLA Ops:
  0.6 0.7 copy-start.1
  2.1 15.9 %copy-start = (bf16[32,512]{1,0:T(8,128)(2,1)S(1)}, bf16[32,512]{1,0:T(8,128)(2,1)}, u32[]{:S(2)}) copy-start(bf16[32,512]{1,0:T(8,128)(2,1)} %samples_ref.1) | copy-start | bytes 98308
  2.1 15.9 %copy-start.2 = (f32[512]{0:T(512)S(1)}, f32[512]{0:T(512)}, u32[]{:S(2)}) copy-start(f32[512]{0:T(512)} %param.5) | copy-start | bytes 6148
  2.1 28.4 %all-to-all-start = ((bf16[16,8,128]{2,1,0:T(8,128)(2,1)}), bf16[16,8,128]{2,1,0:T(8,128)(2,1)S(1)}, u32[]{:S(2)}, u32[]{:S(2)}) async-start(bf16[16,8,128]{2,1,0:T(8,128)(2,1)} %shard_map.58), calls=%async_computation | async-start | bytes 65536 | tf_op jit(solution)/shard_map/all_to_all | solution.py:217
  18.0 9.7 %collective-permute-start.2 = (bf16[40,512]{1,0:T(8,128)(2,1)S(1)}, bf16[40,512]{1,0:T(8,128)(2,1)S(1)}, u32[]{:S(2)}, u32[]{:S(2)}) collective-permute-start(bf16[40,512]{1,0:T(8,128)(2,1)S(1)} %shard_map.59.own_ref), channel_id=1, source_target_pairs={{0,3},{1,2},{2,1},{3,0},{4,7},{5,6},{6,5},{7,4},{8,11},{9,10},{10,... | collective-permute-start | bytes 122888 | tf_op jit(solution)/shard_map/ppermute | solution.py:221
  23.5 7.0 %collective-permute-start.1 = (bf16[40,512]{1,0:T(8,128)(2,1)S(1)}, bf16[40,512]{1,0:T(8,128)(2,1)S(1)}, u32[]{:S(2)}, u32[]{:S(2)}) collective-permute-start(bf16[40,512]{1,0:T(8,128)(2,1)S(1)} %shard_map.59.own_ref), channel_id=1, source_target_pairs={{0,2},{2,0},{1,3},{3,1},{4,6},{6,4},{5,7},{7,5},{8,10},{10,8},{9,1... | collective-permute-start | bytes 122888 | tf_op jit(solution)/shard_map/ppermute | solution.py:220
  25.7 4.8 %collective-permute-start = (bf16[40,512]{1,0:T(8,128)(2,1)S(1)}, bf16[40,512]{1,0:T(8,128)(2,1)S(1)}, u32[]{:S(2)}, u32[]{:S(2)}) collective-permute-start(bf16[40,512]{1,0:T(8,128)(2,1)S(1)} %shard_map.59.own_ref), channel_id=1, source_target_pairs={{0,1},{1,0},{2,3},{3,2},{4,5},{5,4},{6,7},{7,6},{8,9},{9,8},{10,11... | collective-permute-start | bytes 122888 | tf_op jit(solution)/shard_map/ppermute | solution.py:219

commit v4 on v3

--- a/solution.py
+++ b/solution.py
@@ -88,7 +88,7 @@
     samples_out[32:, :] = block.astype(BF16)
 
 
-def row_pass(points_ref, own_ref, core_ref, side_ref, both_ref, x_out, y_out, lse_out):
+def row_pass(points_ref, samples_ref, x_out, y_out, lse_out):
     packed = points_ref[...].astype(F32)
     x = jnp.concatenate(
         [packed.reshape(16, 1, 8, LANES)]
@@ -103,13 +103,7 @@
         x = jnp.where(lane == 35 + k, part, x)
     x = x[:, :DEPTH].astype(BF16)
     x_out[...] = x
-    side = lax.axis_index("x_hi") == 1
-    core = lax.axis_index("core") == 1
-    blocks = [ref[...].astype(F32) for ref in (own_ref, core_ref, side_ref, both_ref)]
-    swap = [blocks[1], blocks[0], blocks[3], blocks[2]]
-    blocks = [jnp.where(core, b, a) for a, b in zip(blocks, swap)]
-    swap = blocks[2:] + blocks[:2]
-    y = jnp.concatenate([jnp.where(side, b, a) for a, b in zip(blocks, swap)], axis=1)
+    y = jnp.concatenate([samples_ref[k].astype(F32) for k in range(4)], axis=1)
     pot = jnp.sum(y[32:40], axis=0, keepdims=True)
     y = y[:32]
     y_norm = -0.5 * jnp.sum(y * y, axis=0, keepdims=True)
@@ -117,16 +111,16 @@
     y_out[:32, :] = y.astype(BF16)
     y_out[32:, :] = extra_rows(y_norm)
     y = jnp.concatenate([y.astype(BF16), extra_rows(y_norm + pot - shift)], axis=0)
+    total = jnp.zeros((POINTS, LANES), F32)
+    for chunk in range(8):
+        right = y[:, chunk * 256 : chunk * 256 + 256]
+        part = jnp.exp2(jnp.dot(x, right, preferred_element_type=F32) * SCALE)
+        total += part[:, :LANES] + part[:, LANES:]
     lines = []
     for tile in range(4):
-        total = jnp.zeros((LANES, LANES), F32)
-        left = x[tile * 128 : tile * 128 + 128]
-        for chunk in range(8):
-            right = y[:, chunk * 256 : chunk * 256 + 256]
-            part = jnp.exp2(jnp.dot(left, right, preferred_element_type=F32) * SCALE)
-            total += part[:, :LANES] + part[:, LANES:]
-        total = jnp.sum(jnp.transpose(total), axis=0, keepdims=True)
-        lines.append(jnp.log2(total) + SCALE * shift)
+        line = jnp.transpose(total[tile * 128 : tile * 128 + 128])
+        line = jnp.sum(line, axis=0, keepdims=True)
+        lines.append(jnp.log2(line) + SCALE * shift)
     lse_out[...] = jnp.broadcast_to(stack_up(lines)[None], (16, 4, LANES))
 
 
@@ -148,12 +142,9 @@
     x_out[...] = x
     lines = []
     for chunk in range(8):
-        total = jnp.zeros((8, 256), F32)
         right = y_ref[:, chunk * 256 : chunk * 256 + 256]
-        for tile in range(4):
-            left = x[tile * 128 : tile * 128 + 128]
-            part = jnp.exp2(jnp.dot(left, right, preferred_element_type=F32) * SCALE)
-            total += jnp.sum(part.reshape(16, 8, 256), axis=0)
+        part = jnp.exp2(jnp.dot(x, right, preferred_element_type=F32) * SCALE)
+        total = jnp.sum(part.reshape(64, 8, 256), axis=0)
         total = jnp.log2(jnp.sum(total, axis=0, keepdims=True)) + SCALE * shift
         lines += [total[:, :LANES], total[:, LANES:]]
     lse_out[...] = jnp.broadcast_to(stack_up(lines)[None], (32, 16, LANES))
@@ -171,34 +162,38 @@
     shift = jnp.max(shift_ref[...])
     y_all = jnp.concatenate([y, extra_rows(y_norm + line_up(sample) + shift)], axis=0)
     right = jnp.concatenate([y, y, y, y, jnp.ones((LANES, SAMPLES), BF16)], axis=0)
-    lane = lanes_of((4, 8, LANES))
-    for tile in range(4):
-        x = x_ref[tile * 128 : tile * 128 + 128, :]
-        total = jnp.zeros((LANES, 2 * LANES), F32)
-        for chunk in range(8):
-            cols = slice(chunk * 256, chunk * 256 + 256)
-            weight = jnp.exp2(jnp.dot(x, y_all[:, cols], preferred_element_type=F32) * SCALE)
-            total += lax.dot_general(
-                weight.astype(BF16),
-                right[:, cols],
-                (((1,), (1,)), ((), ())),
-                preferred_element_type=F32,
-            )
-        numer = total[:, :LANES].reshape(4, 4, 8, LANES)
-        denom = total[:, LANES:].reshape(4, 4, 8, LANES)
-        first, second = numer[:, 0], denom[:, 0]
-        for q in range(1, 4):
-            first = jnp.where(lane // 32 == q, numer[:, q], first)
-            second = jnp.where(lane // 32 == q, denom[:, q], second)
-        parts_out[tile * 4 : tile * 4 + 4, :8, :] = first
-        parts_out[tile * 4 : tile * 4 + 4, 8:, :] = second
+    x = x_ref[...]
+    total = jnp.zeros((POINTS, 2 * LANES), F32)
+    for chunk in range(8):
+        cols = slice(chunk * 256, chunk * 256 + 256)
+        weight = jnp.exp2(jnp.dot(x, y_all[:, cols], preferred_element_type=F32) * SCALE)
+        total += lax.dot_general(
+            weight.astype(BF16),
+            right[:, cols],
+            (((1,), (1,)), ((), ())),
+            preferred_element_type=F32,
+        )
+    numer = total[:, :LANES].reshape(16, 4, 8, LANES)
+    denom = total[:, LANES:].reshape(16, 4, 8, LANES)
+    shape = (16, 8, LANES)
+    lane, row = lanes_of(shape), rows_of(shape)
+    first, second = numer[:, 0], jnp.where(lane == row, denom[:, 0], 0.0)
+    for q in range(1, 4):
+        first = jnp.where(lane // 32 == q, numer[:, q], first)
+        second = jnp.where(lane == row + 8 * q, denom[:, q], second)
+    second = jnp.sum(second, axis=1)
+    for peer in range(16):
+        parts_out[9 * peer : 9 * peer + 8, :] = first[peer]
+        parts_out[9 * peer + 8 : 9 * peer + 9, :] = second[peer : peer + 1]
 
 
 def finish(parts_ref, bary_out):
-    total = jnp.sum(parts_ref[...], axis=0)
-    ratio = total[:8] / total[8:]
-    stack = jnp.concatenate([ratio] + [pltpu.roll(ratio, LANES - 32 * q, 1) for q in range(1, 4)], axis=0)
-    bary_out[...] = turned(stack)[:32, :32]
+    numer, denom = parts_ref[:8, :], parts_ref[8:9, :]
+    for peer in range(1, 16):
+        numer = numer + parts_ref[9 * peer : 9 * peer + 8, :]
+        denom = denom + parts_ref[9 * peer + 8 : 9 * peer + 9, :]
+    stack = [numer] + [pltpu.roll(numer, LANES - 32 * q, 1) for q in range(1, 4)]
+    bary_out[...] = turned(jnp.concatenate(stack, axis=0))[:32, :32] / denom[:, :32]
 
 
 def call(body, outs, *args):
@@ -216,13 +211,11 @@
     (xs,) = call(prepare_points, [((16, 8, LANES), BF16)], points)
     xs = lax.all_to_all(xs, "z", 0, 0).reshape(LANES, LANES)
     (own,) = call(prepare_samples, [((40, 512), BF16)], samples, potential.reshape(1, 512))
-    core = lax.ppermute(own, "core", [(0, 1), (1, 0)])
-    side = lax.ppermute(own, "x_hi", [(0, 1), (1, 0)])
-    both = lax.ppermute(own, ("x_hi", "core"), [(k, 3 - k) for k in range(4)])
+    ys = lax.all_gather(own, ("x_hi", "core"))
     x, y, rows = call(
         row_pass,
         [((POINTS, DEPTH), BF16), ((DEPTH, SAMPLES), BF16), ((16, 4, LANES), F32)],
-        xs, own, core, side, both,
+        xs, ys,
     )
     rows = lax.all_to_all(rows, "z", 0, 0)
     x, shift, cols, point = call(
@@ -232,9 +225,10 @@
     )
     cols = lax.all_to_all(cols, PLANE, 0, 0)
     parts, sample = call(
-        weigh, [((16, 16, LANES), F32), ((4, LANES), F32)], x, y, shift, cols
-    )
-    parts = lax.all_to_all(parts, "z", 0, 0)
+        weigh, [((144, LANES), F32), ((4, LANES), F32)], x, y, shift, cols
+    )
+    parts = parts.reshape(16, 9, 1, LANES)
+    parts = lax.all_to_all(parts, "z", 0, 0).reshape(144, LANES)
     (bary,) = call(finish, [((32, 32), F32)], parts)
     return point.reshape(32), sample.reshape(512), bary
 

time: 91.5 us -> 86.1 us (0.941); the launches traced: 89.8 us -> 85.7 us
  starting transfers between devices: 25.6 us -> 15.9 us
  blocking collectives: 53.1 us -> 58.6 us
    ppermute x3 -> x0, starting transfers between devices: 9.72 us -> none  [the longest x1 5.49 us: on_device(): both = lax.ppermute(own, ('x_hi', 'core'), [(k, 3 - k) for k in range(4)])]
    all_gather x0 -> x1, blocking collectives: none -> 7.81 us  [on_device(): ys = lax.all_gather(own, ('x_hi', 'core'))]
    all_to_all x1, waiting for transfers between devices: 0.01 us -> 3.61 us  [on_device(): xs = lax.all_to_all(xs, 'z', 0, 0).reshape(LANES, LANES)]
    all_to_all x1, blocking collectives: 22.5 us -> 19.5 us  [on_device(): rows = lax.all_to_all(rows, 'z', 0, 0)]
    ppermute x3 -> x0, waiting for transfers between devices: 2.72 us -> none  [the longest x1 2.72 us: on_device(): side = lax.ppermute(own, 'x_hi', [(0, 1), (1, 0)])]
    all_to_all x1, blocking collectives: 16 us -> 17.1 us  [on_device(): cols = lax.all_to_all(cols, PLANE, 0, 0)]
  transfers between devices with their start and end apart: 4 -> 1, of which waited for: 1 -> 1; matrix products, arithmetic and copies ran while one was open for 0% -> 0% of each run, Pallas kernels for 0% -> 0%
where the time goes in v4:
time: 86.1 us; the launch traced here: 85.7 us
  blocking collectives  58.6 us (68%)
  starting transfers between devices  15.9 us (18%)
  Pallas kernels  6.27 us (7%)
  waiting for transfers between devices  3.61 us (4%)
    all_to_all x1, blocking collectives, on_device(): rows = lax.all_to_all(rows, 'z', 0, 0)  19.5 us
    all_to_all x1, blocking collectives, on_device(): cols = lax.all_to_all(cols, PLANE, 0, 0)  17.1 us
    all_to_all x1, starting transfers between devices, on_device(): xs = lax.all_to_all(xs, 'z', 0, 0).reshape(LANES, LANES)  15.9 us
    all_to_all x1, blocking collectives, on_device(): parts = lax.all_to_all(parts, 'z', 0, 0).reshape(144, LANES)  14.2 us
    all_gather x1, blocking collectives, on_device(): ys = lax.all_gather(own, ('x_hi', 'core'))  7.81 us
    pallas_call x6, Pallas kernels, call(): pl.pallas_call(body, out_shape=[jax.ShapeDtypeStruct(shape, dtype) for sh...  6.27 us
    all_to_all x1, waiting for transfers between devices, on_device(): xs = lax.all_to_all(xs, 'z', 0, 0).reshape(LANES, LANES)  3.61 us
  transfers between devices with their start and end apart: 1, of which 1 were waited for; matrix products, arithmetic and copies ran while one was open for 0% of the time, Pallas kernels for 0%

profile of v4, /device:TPU:1, one launch (start us, length us, event | category | flops | bytes accessed | tf_op | source)
XLA Modules:
  0.0 85.7 jit_solution(15800813078417778153)
XLA Ops:
  0.6 0.0 copy-start.1
  0.6 0.7 copy-done.1
  1.3 0.7 shard_map.58
  2.1 0.0 copy-start
  2.1 0.0 copy-start.2
  2.1 15.9 %all-to-all-start = ((bf16[16,8,128]{2,1,0:T(8,128)(2,1)}), bf16[16,8,128]{2,1,0:T(8,128)(2,1)S(1)}, u32[]{:S(2)}, u32[]{:S(2)}) async-start(bf16[16,8,128]{2,1,0:T(8,128)(2,1)} %shard_map.58), calls=%async_computation | async-start | bytes 65536 | tf_op jit(solution)/shard_map/all_to_all | solution.py:212
  18.0 0.0 copy-done
  18.0 0.0 copy-done.2
  18.0 7.8 %all-gather = bf16[160,512]{1,0:T(8,128)(2,1)S(1)} all-gather(bf16[40,512]{1,0:T(8,128)(2,1)S(1)} %shard_map.59), channel_id=2, replica_groups=mesh['x_lo'=2,'y'=4,'z'=16,'x_hi'=2,'core'=2] {'x_hi','core'}, dimensions={0}, use_global_device_ids=true | all-gather | bytes 204800 | tf_op jit(solution)/shard_map/all_gather | solution.py:214
  25.8 3.6 %all-to-all-done = bf16[16,8,128]{2,1,0:T(8,128)(2,1)S(1)} async-done(((bf16[16,8,128]{2,1,0:T(8,128)(2,1)}), bf16[16,8,128]{2,1,0:T(8,128)(2,1)S(1)}, u32[]{:S(2)}, u32[]{:S(2)}) %all-to-all-start) | async-done | bytes 32800 | tf_op jit(solution)/shard_map/all_to_all | solution.py:212
  29.4 1.1 %shard_map.60 = (bf16[512,48]{1,0:T(8,128)(2,1)S(1)}, bf16[48,2048]{1,0:T(8,128)(2,1)S(1)}, f32[16,4,128]{2,1,0:T(4,128)S(1)}) custom-call(bf16[128,128]{1,0:T(8,128)(2,1)S(1)} %bitcast.9, bf16[4,40,512]{2,1,0:T(8,128)(2,1)S(1)} %bitcast.7), custom_call_target="tpu_custom_call" | custom-call | tf_op jit(solution)/shard_map/pallas_call | solution.py:201
  30.6 19.5 %all_to_all.20.rows_ref = f32[16,4,128]{2,1,0:T(4,128)S(1)} all-to-all(f32[16,4,128]{2,1,0:T(4,128)S(1)} %get-tuple-element.14), channel_id=1, replica_groups=mesh['x_lo'=2,'y'=4,'z'=16,'x_hi'=2,'core'=2] {'z'}, dimensions={0} | all-to-all | bytes 65536 | tf_op jit(solution)/shard_map/all_to_all | solution.py:220
  50.1 1.6 %shard_map.61 = (bf16[512,48]{1,0:T(8,128)(2,1)S(1)}, f32[1,128]{1,0:T(1,128)S(1)}, f32[32,16,128]{2,1,0:T(8,128)S(1)}, f32[1,32]{1,0:T(1,128)}) custom-call(bf16[512,48]{1,0:T(8,128)(2,1)S(1)} %get-tuple-element.12.x_ref, bf16[48,2048]{1,0:T(8,128)(2,1)S(1)} %get-tuple-element.13.y_ref, f32[16,4,128]{2,1,0:T(4,128)S(1)} %all_to_all.20.rows_ref), custom_call_target="tpu_custom_call" | custom-call | tf_op jit(solution)/shard_map/pallas_call | solution.py:201
  51.7 17.1 %all_to_all.21.cols_ref = f32[32,16,128]{2,1,0:T(8,128)S(1)} all-to-all(f32[32,16,128]{2,1,0:T(8,128)S(1)} %get-tuple-element.18), channel_id=1, replica_groups=mesh['x_lo'=2,'y'=4,'z'=16,'x_hi'=2,'core'=2] {'x_lo','y','x_hi','core'}, dimensions={0} | all-to-all | bytes 524288 | tf_op jit(solution)/shard_map/all_to_all | solution.py:226
  68.8 2.0 %shard_map.62 = (f32[144,128]{1,0:T(8,128)S(1)}, f32[4,128]{1,0:T(4,128)}) custom-call(bf16[512,48]{1,0:T(8,128)(2,1)S(1)} %get-tuple-element.16.x_ref, bf16[48,2048]{1,0:T(8,128)(2,1)S(1)} %get-tuple-element.13.y_ref, f32[1,128]{1,0:T(1,128)S(1)} %get-tuple-element.17.shift_ref, f32[32,16,128]{2,1,0:T(8,128)S(1)} %all_to_all.21.cols_ref), custom_call_target="tpu_custom_call" | custom-call | tf_op jit(solution)/shard_map/pallas_call | solution.py:201
  70.8 14.2 %all_to_all.22 = f32[16,9,1,128]{3,2,1,0:T(1,128)S(1)} all-to-all(f32[16,9,1,128]{3,2,1,0:T(1,128)S(1)} %bitcast.10), channel_id=1, replica_groups=mesh['x_lo'=2,'y'=4,'z'=16,'x_hi'=2,'core'=2] {'z'}, dimensions={0} | all-to-all | bytes 147456 | tf_op jit(solution)/shard_map/all_to_all | solution.py:231
  85.0 0.8 shard_map.63
  (1 shorter events, 0.0 us)
Async XLA Ops:
  0.6 0.7 copy-start.1
  2.1 15.9 %copy-start = (bf16[32,512]{1,0:T(8,128)(2,1)S(1)}, bf16[32,512]{1,0:T(8,128)(2,1)}, u32[]{:S(2)}) copy-start(bf16[32,512]{1,0:T(8,128)(2,1)} %samples_ref.1) | copy-start | bytes 98308
  2.1 15.9 %copy-start.2 = (f32[512]{0:T(512)S(1)}, f32[512]{0:T(512)}, u32[]{:S(2)}) copy-start(f32[512]{0:T(512)} %param.5) | copy-start | bytes 6148
  2.1 27.4 %all-to-all-start = ((bf16[16,8,128]{2,1,0:T(8,128)(2,1)}), bf16[16,8,128]{2,1,0:T(8,128)(2,1)S(1)}, u32[]{:S(2)}, u32[]{:S(2)}) async-start(bf16[16,8,128]{2,1,0:T(8,128)(2,1)} %shard_map.58), calls=%async_computation | async-start | bytes 65536 | tf_op jit(solution)/shard_map/all_to_all | solution.py:212

commit v5 on v4

--- a/solution.py
+++ b/solution.py
@@ -126,7 +126,7 @@
 
 def col_pass(x_ref, y_ref, rows_ref, x_out, shift_out, lse_out, own_out):
     point = (LOG_SAMPLES - combine(rows_ref[...])) / SCALE
-    z = lax.axis_index("z")
+    z = (lax.axis_index("z") + 6) % 16
     line = jnp.sum(jnp.where(rows_of(point.shape) == z // 4, point, 0.0), axis=0, keepdims=True)
     line = pltpu.roll(jnp.broadcast_to(line, (8, LANES)), (4 - z % 4) * 32 % LANES, 1)
     own_out[...] = line[:1, :32]
@@ -196,6 +196,12 @@
     bary_out[...] = turned(jnp.concatenate(stack, axis=0))[:32, :32] / denom[:, :32]
 
 
+def exchange(value, axes, first):
+    count = lax.axis_size(axes)
+    order = [(first + k) % count for k in range(count)]
+    return lax.all_to_all(value, axes, 0, 0, axis_index_groups=[order])
+
+
 def call(body, outs, *args):
     vmem = pl.BlockSpec(memory_space=pltpu.VMEM)
     return pl.pallas_call(
@@ -209,7 +215,7 @@
 
 def on_device(points, samples, potential):
     (xs,) = call(prepare_points, [((16, 8, LANES), BF16)], points)
-    xs = lax.all_to_all(xs, "z", 0, 0).reshape(LANES, LANES)
+    xs = exchange(xs, "z", 10).reshape(LANES, LANES)
     (own,) = call(prepare_samples, [((40, 512), BF16)], samples, potential.reshape(1, 512))
     ys = lax.all_gather(own, ("x_hi", "core"))
     x, y, rows = call(
@@ -217,18 +223,18 @@
         [((POINTS, DEPTH), BF16), ((DEPTH, SAMPLES), BF16), ((16, 4, LANES), F32)],
         xs, ys,
     )
-    rows = lax.all_to_all(rows, "z", 0, 0)
+    rows = exchange(rows, "z", 10)
     x, shift, cols, point = call(
         col_pass,
         [((POINTS, DEPTH), BF16), ((1, LANES), F32), ((32, 16, LANES), F32), ((1, 32), F32)],
         x, y, rows,
     )
-    cols = lax.all_to_all(cols, PLANE, 0, 0)
+    cols = exchange(cols, PLANE, 10)
     parts, sample = call(
         weigh, [((144, LANES), F32), ((4, LANES), F32)], x, y, shift, cols
     )
     parts = parts.reshape(16, 9, 1, LANES)
-    parts = lax.all_to_all(parts, "z", 0, 0).reshape(144, LANES)
+    parts = exchange(parts, "z", 10).reshape(144, LANES)
     (bary,) = call(finish, [((32, 32), F32)], parts)
     return point.reshape(32), sample.reshape(512), bary
 

time: 86.1 us -> 78.8 us (0.915)
  blocking collectives: 58.6 us -> 53.4 us
  waiting for transfers between devices: 3.61 us -> 0.01 us
  starting transfers between devices: 15.9 us -> 17.5 us
    all_to_all x3, blocking collectives: 50.8 us -> 45.3 us  [exchange(): return lax.all_to_all(value, axes, 0, 0, axis_index_groups=[order])]
    all_to_all x1, waiting for transfers between devices: 3.61 us -> 0.01 us  [exchange(): return lax.all_to_all(value, axes, 0, 0, axis_index_groups=[order])]
    all_to_all x1, starting transfers between devices: 15.9 us -> 17.5 us  [exchange(): return lax.all_to_all(value, axes, 0, 0, axis_index_groups=[order])]
  transfers between devices with their start and end apart: 1 -> 1, of which waited for: 1 -> 0; matrix products, arithmetic and copies ran while one was open for 0% -> 0% of each run, Pallas kernels for 0% -> 0%
where the time goes in v5:
time: 78.8 us; the launch traced here: 78.5 us
  blocking collectives  53.4 us (68%)
  starting transfers between devices  17.5 us (22%)
  Pallas kernels  6.27 us (8%)
    all_to_all x3, blocking collectives, exchange(): return lax.all_to_all(value, axes, 0, 0, axis_index_groups=[order])  45.3 us
    all_to_all x1, starting transfers between devices, exchange(): return lax.all_to_all(value, axes, 0, 0, axis_index_groups=[order])  17.5 us
    all_gather x1, blocking collectives, on_device(): ys = lax.all_gather(own, ('x_hi', 'core'))  8.09 us
    pallas_call x6, Pallas kernels, call(): pl.pallas_call(body, out_shape=[jax.ShapeDtypeStruct(shape, dtype) for sh...  6.27 us
  transfers between devices with their start and end apart: 1, of which 0 were waited for; matrix products, arithmetic and copies ran while one was open for 0% of the time, Pallas kernels for 0%

profile of v5, /device:TPU:1, one launch (start us, length us, event | category | flops | bytes accessed | tf_op | source)
XLA Modules:
  0.0 78.5 jit_solution(5611071522618104118)
XLA Ops:
  0.6 0.0 copy-start.1
  0.6 0.7 copy-done.1
  1.3 0.7 shard_map.58
  2.1 0.0 copy-start
  2.1 0.0 copy-start.2
  2.1 17.5 %all-to-all-start = ((bf16[16,8,128]{2,1,0:T(8,128)(2,1)}), bf16[16,8,128]{2,1,0:T(8,128)(2,1)S(1)}, u32[]{:S(2)}, u32[]{:S(2)}) async-start(bf16[16,8,128]{2,1,0:T(8,128)(2,1)} %shard_map.58), calls=%async_computation | async-start | bytes 65536 | tf_op jit(solution)/shard_map/all_to_all | solution.py:202
  19.5 0.0 copy-done
  19.5 0.0 copy-done.2
  19.6 8.1 %all-gather = bf16[160,512]{1,0:T(8,128)(2,1)S(1)} all-gather(bf16[40,512]{1,0:T(8,128)(2,1)S(1)} %shard_map.59), channel_id=2, replica_groups=mesh['x_lo'=2,'y'=4,'z'=16,'x_hi'=2,'core'=2] {'x_hi','core'}, dimensions={0}, use_global_device_ids=true | all-gather | bytes 204800 | tf_op jit(solution)/shard_map/all_gather | solution.py:220
  27.7 0.0 all-to-all-done
  27.7 1.1 %shard_map.60 = (bf16[512,48]{1,0:T(8,128)(2,1)S(1)}, bf16[48,2048]{1,0:T(8,128)(2,1)S(1)}, f32[16,4,128]{2,1,0:T(4,128)S(1)}) custom-call(bf16[128,128]{1,0:T(8,128)(2,1)S(1)} %bitcast.9, bf16[4,40,512]{2,1,0:T(8,128)(2,1)S(1)} %bitcast.7), custom_call_target="tpu_custom_call" | custom-call | tf_op jit(solution)/shard_map/pallas_call | solution.py:207
  28.8 15.5 %all_to_all.20.rows_ref = f32[16,4,128]{2,1,0:T(4,128)S(1)} all-to-all(f32[16,4,128]{2,1,0:T(4,128)S(1)} %get-tuple-element.14), channel_id=1, replica_groups={{40,44,48,52,56,60,0,4,8,12,16,20,24,28,32,36},{41,45,49,53,57,61,1,5,9..., dimensions={0} | all-to-all | bytes 65536 | tf_op jit(solution)/shard_map/all_to_all | solution.py:202
  44.3 1.6 %shard_map.61 = (bf16[512,48]{1,0:T(8,128)(2,1)S(1)}, f32[1,128]{1,0:T(1,128)S(1)}, f32[32,16,128]{2,1,0:T(8,128)S(1)}, f32[1,32]{1,0:T(1,128)}) custom-call(bf16[512,48]{1,0:T(8,128)(2,1)S(1)} %get-tuple-element.12.x_ref, bf16[48,2048]{1,0:T(8,128)(2,1)S(1)} %get-tuple-element.13.y_ref, f32[16,4,128]{2,1,0:T(4,128)S(1)} %all_to_all.20.rows_ref), custom_call_target="tpu_custom_call" | custom-call | tf_op jit(solution)/shard_map/pallas_call | solution.py:207
  45.9 13.9 %all_to_all.21.cols_ref = f32[32,16,128]{2,1,0:T(8,128)S(1)} all-to-all(f32[32,16,128]{2,1,0:T(8,128)S(1)} %get-tuple-element.18), channel_id=1, replica_groups={{130,131,192,193,194,195,256,257,258,259,320,321,322,323,384,385,386,38..., dimensions={0} | all-to-all | bytes 524288 | tf_op jit(solution)/shard_map/all_to_all | solution.py:202
  59.8 2.0 %shard_map.62 = (f32[144,128]{1,0:T(8,128)S(1)}, f32[4,128]{1,0:T(4,128)}) custom-call(bf16[512,48]{1,0:T(8,128)(2,1)S(1)} %get-tuple-element.16.x_ref, bf16[48,2048]{1,0:T(8,128)(2,1)S(1)} %get-tuple-element.13.y_ref, f32[1,128]{1,0:T(1,128)S(1)} %get-tuple-element.17.shift_ref, f32[32,16,128]{2,1,0:T(8,128)S(1)} %all_to_all.21.cols_ref), custom_call_target="tpu_custom_call" | custom-call | tf_op jit(solution)/shard_map/pallas_call | solution.py:207
  61.8 15.9 %all_to_all.22 = f32[16,9,1,128]{3,2,1,0:T(1,128)S(1)} all-to-all(f32[16,9,1,128]{3,2,1,0:T(1,128)S(1)} %bitcast.10), channel_id=1, replica_groups={{40,44,48,52,56,60,0,4,8,12,16,20,24,28,32,36},{41,45,49,53,57,61,1,5,9..., dimensions={0} | all-to-all | bytes 147456 | tf_op jit(solution)/shard_map/all_to_all | solution.py:202
  77.7 0.8 shard_map.63
  (1 shorter events, 0.0 us)
Async XLA Ops:
  0.6 0.7 copy-start.1
  2.1 17.5 %copy-start = (bf16[32,512]{1,0:T(8,128)(2,1)S(1)}, bf16[32,512]{1,0:T(8,128)(2,1)}, u32[]{:S(2)}) copy-start(bf16[32,512]{1,0:T(8,128)(2,1)} %samples_ref.1) | copy-start | bytes 98308
  2.1 17.5 %copy-start.2 = (f32[512]{0:T(512)S(1)}, f32[512]{0:T(512)}, u32[]{:S(2)}) copy-start(f32[512]{0:T(512)} %param.5) | copy-start | bytes 6148
  2.1 25.6 %all-to-all-start = ((bf16[16,8,128]{2,1,0:T(8,128)(2,1)}), bf16[16,8,128]{2,1,0:T(8,128)(2,1)S(1)}, u32[]{:S(2)}, u32[]{:S(2)}) async-start(bf16[16,8,128]{2,1,0:T(8,128)(2,1)} %shard_map.58), calls=%async_computation | async-start | bytes 65536 | tf_op jit(solution)/shard_map/all_to_all | solution.py:202

commit v6 on v4

--- a/solution.py
+++ b/solution.py
@@ -43,6 +43,10 @@
     if rows < LANES:
         block = jnp.concatenate([block, jnp.zeros((LANES - rows, cols), block.dtype)], axis=0)
     return jnp.transpose(block)
+
+
+def product(left, right):
+    return lax.dot_general(left, right, (((1,), (1,)), ((), ())), preferred_element_type=F32)
 
 
 def combine(lse):
@@ -111,14 +115,15 @@
     y_out[:32, :] = y.astype(BF16)
     y_out[32:, :] = extra_rows(y_norm)
     y = jnp.concatenate([y.astype(BF16), extra_rows(y_norm + pot - shift)], axis=0)
-    total = jnp.zeros((POINTS, LANES), F32)
-    for chunk in range(8):
-        right = y[:, chunk * 256 : chunk * 256 + 256]
-        part = jnp.exp2(jnp.dot(x, right, preferred_element_type=F32) * SCALE)
-        total += part[:, :LANES] + part[:, LANES:]
     lines = []
     for tile in range(4):
-        line = jnp.transpose(total[tile * 128 : tile * 128 + 128])
+        total = jnp.zeros((LANES, LANES), F32)
+        left = x[tile * 128 : tile * 128 + 128]
+        for chunk in range(8):
+            right = y[:, chunk * 256 : chunk * 256 + 256]
+            part = jnp.exp2(jnp.dot(left, right, preferred_element_type=F32) * SCALE)
+            total += part[:, :LANES] + part[:, LANES:]
+        line = jnp.transpose(total)
         line = jnp.sum(line, axis=0, keepdims=True)
         lines.append(jnp.log2(line) + SCALE * shift)
     lse_out[...] = jnp.broadcast_to(stack_up(lines)[None], (16, 4, LANES))
@@ -127,24 +132,30 @@
 def col_pass(x_ref, y_ref, rows_ref, x_out, shift_out, lse_out, own_out):
     point = (LOG_SAMPLES - combine(rows_ref[...])) / SCALE
     z = lax.axis_index("z")
+    z = sum(jnp.where(z == other, slot, 0) for slot, other in enumerate(Z_ORDER))
     line = jnp.sum(jnp.where(rows_of(point.shape) == z // 4, point, 0.0), axis=0, keepdims=True)
     line = pltpu.roll(jnp.broadcast_to(line, (8, LANES)), (4 - z % 4) * 32 % LANES, 1)
     own_out[...] = line[:1, :32]
     shift = jnp.max(point) - MARGIN
     shift_out[...] = jnp.full((1, LANES), shift, F32)
-    flipped = turned(point - shift)
-    x = x_ref[...].astype(F32)
-    column = jnp.concatenate([flipped[:, k : k + 1] for k in range(4)], axis=0)
-    lane = lanes_of(x.shape)
-    for k, part in enumerate(triple(column)):
-        x = jnp.where(lane == 38 + k, part, x)
-    x = x.astype(BF16)
+    parts = triple(point - shift)
+    row = rows_of((DEPTH, LANES))
+    blocks = []
+    for tile in range(4):
+        block = jnp.zeros((DEPTH, LANES), F32)
+        for k, part in enumerate(parts):
+            block = jnp.where(row == 38 + k, part[tile : tile + 1], block)
+        blocks.append(jnp.transpose(block))
+    x = (x_ref[...].astype(F32) + jnp.concatenate(blocks, axis=0)).astype(BF16)
     x_out[...] = x
     lines = []
     for chunk in range(8):
         right = y_ref[:, chunk * 256 : chunk * 256 + 256]
-        part = jnp.exp2(jnp.dot(x, right, preferred_element_type=F32) * SCALE)
-        total = jnp.sum(part.reshape(64, 8, 256), axis=0)
+        total = jnp.zeros((8, 256), F32)
+        for tile in range(4):
+            left = x[tile * 128 : tile * 128 + 128]
+            part = jnp.exp2(jnp.dot(left, right, preferred_element_type=F32) * SCALE)
+            total += jnp.sum(part.reshape(16, 8, 256), axis=0)
         total = jnp.log2(jnp.sum(total, axis=0, keepdims=True)) + SCALE * shift
         lines += [total[:, :LANES], total[:, LANES:]]
     lse_out[...] = jnp.broadcast_to(stack_up(lines)[None], (32, 16, LANES))
@@ -161,30 +172,29 @@
     y_norm = jnp.sum(y_ref[32:, :].astype(F32)[:3], axis=0, keepdims=True)
     shift = jnp.max(shift_ref[...])
     y_all = jnp.concatenate([y, extra_rows(y_norm + line_up(sample) + shift)], axis=0)
-    right = jnp.concatenate([y, y, y, y, jnp.ones((LANES, SAMPLES), BF16)], axis=0)
     x = x_ref[...]
-    total = jnp.zeros((POINTS, 2 * LANES), F32)
-    for chunk in range(8):
-        cols = slice(chunk * 256, chunk * 256 + 256)
-        weight = jnp.exp2(jnp.dot(x, y_all[:, cols], preferred_element_type=F32) * SCALE)
-        total += lax.dot_general(
-            weight.astype(BF16),
-            right[:, cols],
-            (((1,), (1,)), ((), ())),
-            preferred_element_type=F32,
-        )
-    numer = total[:, :LANES].reshape(16, 4, 8, LANES)
-    denom = total[:, LANES:].reshape(16, 4, 8, LANES)
-    shape = (16, 8, LANES)
+    right = jnp.concatenate([y, y, y, y, jnp.ones((128, SAMPLES), BF16)], axis=0)
+    shape = (8, 8, LANES)
     lane, row = lanes_of(shape), rows_of(shape)
-    first, second = numer[:, 0], jnp.where(lane == row, denom[:, 0], 0.0)
-    for q in range(1, 4):
-        first = jnp.where(lane // 32 == q, numer[:, q], first)
-        second = jnp.where(lane == row + 8 * q, denom[:, q], second)
-    second = jnp.sum(second, axis=1)
-    for peer in range(16):
-        parts_out[9 * peer : 9 * peer + 8, :] = first[peer]
-        parts_out[9 * peer + 8 : 9 * peer + 9, :] = second[peer : peer + 1]
+    for tile in range(2):
+        weights = []
+        for chunk in range(8):
+            cols = slice(chunk * 256, chunk * 256 + 256)
+            part = jnp.dot(x[tile * 256 : tile * 256 + 256], y_all[:, cols], preferred_element_type=F32)
+            weights.append(jnp.exp2(part * SCALE).astype(BF16))
+        total = product(jnp.concatenate(weights, axis=1), right)
+        numer = total[:, :LANES].reshape(8, 4, 8, LANES)
+        denom = total[:, LANES:]
+        denom = denom.reshape(8, 4, 8, 128)
+        first, second = numer[:, 0], jnp.where(lane[:, :, :128] == row[:, :, :128], denom[:, 0], 0.0)
+        for q in range(1, 4):
+            first = jnp.where(lane // 32 == q, numer[:, q], first)
+            second = jnp.where(lane[:, :, :128] == row[:, :, :128] + 8 * q, denom[:, q], second)
+        second = jnp.sum(second, axis=1)
+        for part in range(8):
+            peer = tile * 8 + part
+            parts_out[9 * peer : 9 * peer + 8, :] = first[part]
+            parts_out[9 * peer + 8 : 9 * peer + 9, :128] = second[part : part + 1]
 
 
 def finish(parts_ref, bary_out):
@@ -194,6 +204,14 @@
         denom = denom + parts_ref[9 * peer + 8 : 9 * peer + 9, :]
     stack = [numer] + [pltpu.roll(numer, LANES - 32 * q, 1) for q in range(1, 4)]
     bary_out[...] = turned(jnp.concatenate(stack, axis=0))[:32, :32] / denom[:, :32]
+
+
+Z_ORDER = (10, 11, 9, 12, 8, 13, 7, 14, 6, 15, 5, 0, 4, 1, 3, 2)
+PLANE_ORDER = (10, 11, 12, 13, 14, 15, 16, 17, 18, 19, 20, 21, 22, 23, 24, 25, 26, 27, 28, 29, 30, 31, 0, 1, 2, 3, 4, 5, 6, 7, 8, 9)
+
+
+def exchange(value, axes, order):
+    return lax.all_to_all(value, axes, 0, 0, axis_index_groups=[list(order)])
 
 
 def call(body, outs, *args):
@@ -209,7 +227,7 @@
 
 def on_device(points, samples, potential):
     (xs,) = call(prepare_points, [((16, 8, LANES), BF16)], points)
-    xs = lax.all_to_all(xs, "z", 0, 0).reshape(LANES, LANES)
+    xs = exchange(xs, "z", Z_ORDER).reshape(LANES, LANES)
     (own,) = call(prepare_samples, [((40, 512), BF16)], samples, potential.reshape(1, 512))
     ys = lax.all_gather(own, ("x_hi", "core"))
     x, y, rows = call(
@@ -217,18 +235,18 @@
         [((POINTS, DEPTH), BF16), ((DEPTH, SAMPLES), BF16), ((16, 4, LANES), F32)],
         xs, ys,
     )
-    rows = lax.all_to_all(rows, "z", 0, 0)
+    rows = exchange(rows, "z", Z_ORDER)
     x, shift, cols, point = call(
         col_pass,
         [((POINTS, DEPTH), BF16), ((1, LANES), F32), ((32, 16, LANES), F32), ((1, 32), F32)],
         x, y, rows,
     )
-    cols = lax.all_to_all(cols, PLANE, 0, 0)
+    cols = exchange(cols, PLANE, PLANE_ORDER)
     parts, sample = call(
         weigh, [((144, LANES), F32), ((4, LANES), F32)], x, y, shift, cols
     )
     parts = parts.reshape(16, 9, 1, LANES)
-    parts = lax.all_to_all(parts, "z", 0, 0).reshape(144, LANES)
+    parts = exchange(parts, "z", Z_ORDER).reshape(144, LANES)
     (bary,) = call(finish, [((32, 32), F32)], parts)
     return point.reshape(32), sample.reshape(512), bary
 

time: 86.1 us -> 78 us (0.906)
  blocking collectives: 58.6 us -> 52.8 us
  waiting for transfers between devices: 3.61 us -> 0.01 us
  starting transfers between devices: 15.9 us -> 17.5 us
    all_to_all x3, blocking collectives: 50.8 us -> 44.7 us  [exchange(): return lax.all_to_all(value, axes, 0, 0, axis_index_groups=[list(order)])]
    all_to_all x1, waiting for transfers between devices: 3.61 us -> 0.01 us  [exchange(): return lax.all_to_all(value, axes, 0, 0, axis_index_groups=[list(order)])]
    all_to_all x1, starting transfers between devices: 15.9 us -> 17.5 us  [exchange(): return lax.all_to_all(value, axes, 0, 0, axis_index_groups=[list(order)])]
  transfers between devices with their start and end apart: 1 -> 1, of which waited for: 1 -> 0; matrix products, arithmetic and copies ran while one was open for 0% -> 0% of each run, Pallas kernels for 0% -> 0%
where the time goes in v6:
time: 78 us; the launch traced here: 77.5 us
  blocking collectives  52.8 us (68%)
  starting transfers between devices  17.5 us (22%)
  Pallas kernels  5.91 us (8%)
    all_to_all x3, blocking collectives, exchange(): return lax.all_to_all(value, axes, 0, 0, axis_index_groups=[list(order)])  44.7 us
    all_to_all x1, starting transfers between devices, exchange(): return lax.all_to_all(value, axes, 0, 0, axis_index_groups=[list(order)])  17.5 us
    all_gather x1, blocking collectives, on_device(): ys = lax.all_gather(own, ('x_hi', 'core'))  8.09 us
    pallas_call x6, Pallas kernels, call(): pl.pallas_call(body, out_shape=[jax.ShapeDtypeStruct(shape, dtype) for sh...  5.91 us
  transfers between devices with their start and end apart: 1, of which 0 were waited for; matrix products, arithmetic and copies ran while one was open for 0% of the time, Pallas kernels for 0%

profile of v6, /device:TPU:1, one launch (start us, length us, event | category | flops | bytes accessed | tf_op | source)
XLA Modules:
  0.0 77.5 jit_solution(2634966144864663111)
XLA Ops:
  0.6 0.0 copy-start.1
  0.6 0.7 copy-done.1
  1.3 0.7 shard_map.58
  2.1 0.0 copy-start
  2.1 0.0 copy-start.2
  2.1 17.5 %all-to-all-start = ((bf16[16,8,128]{2,1,0:T(8,128)(2,1)}), bf16[16,8,128]{2,1,0:T(8,128)(2,1)S(1)}, u32[]{:S(2)}, u32[]{:S(2)}) async-start(bf16[16,8,128]{2,1,0:T(8,128)(2,1)} %shard_map.58), calls=%async_computation | async-start | bytes 65536 | tf_op jit(solution)/shard_map/all_to_all | solution.py:214
  19.5 0.0 copy-done
  19.5 0.0 copy-done.2
  19.6 8.1 %all-gather = bf16[160,512]{1,0:T(8,128)(2,1)S(1)} all-gather(bf16[40,512]{1,0:T(8,128)(2,1)S(1)} %shard_map.59), channel_id=2, replica_groups=mesh['x_lo'=2,'y'=4,'z'=16,'x_hi'=2,'core'=2] {'x_hi','core'}, dimensions={0}, use_global_device_ids=true | all-gather | bytes 204800 | tf_op jit(solution)/shard_map/all_gather | solution.py:232
  27.7 0.0 all-to-all-done
  27.7 1.0 %shard_map.60 = (bf16[512,48]{1,0:T(8,128)(2,1)S(1)}, bf16[48,2048]{1,0:T(8,128)(2,1)S(1)}, f32[16,4,128]{2,1,0:T(4,128)S(1)}) custom-call(bf16[128,128]{1,0:T(8,128)(2,1)S(1)} %bitcast.9, bf16[4,40,512]{2,1,0:T(8,128)(2,1)S(1)} %bitcast.7), custom_call_target="tpu_custom_call" | custom-call | tf_op jit(solution)/shard_map/pallas_call | solution.py:219
  28.7 15.5 %all_to_all.20.rows_ref = f32[16,4,128]{2,1,0:T(4,128)S(1)} all-to-all(f32[16,4,128]{2,1,0:T(4,128)S(1)} %get-tuple-element.14), channel_id=1, replica_groups={{40,44,36,48,32,52,28,56,24,60,20,0,16,4,12,8},{41,45,37,49,33,53,29,57..., dimensions={0} | all-to-all | bytes 65536 | tf_op jit(solution)/shard_map/all_to_all | solution.py:214
  44.1 1.4 %shard_map.61 = (bf16[512,48]{1,0:T(8,128)(2,1)S(1)}, f32[1,128]{1,0:T(1,128)S(1)}, f32[32,16,128]{2,1,0:T(8,128)S(1)}, f32[1,32]{1,0:T(1,128)}) custom-call(bf16[512,48]{1,0:T(8,128)(2,1)S(1)} %get-tuple-element.12.x_ref, bf16[48,2048]{1,0:T(8,128)(2,1)S(1)} %get-tuple-element.13.y_ref, f32[16,4,128]{2,1,0:T(4,128)S(1)} %all_to_all.20.rows_ref), custom_call_target="tpu_custom_call" | custom-call | tf_op jit(solution)/shard_map/pallas_call | solution.py:219
  45.5 13.9 %all_to_all.21.cols_ref = f32[32,16,128]{2,1,0:T(8,128)S(1)} all-to-all(f32[32,16,128]{2,1,0:T(8,128)S(1)} %get-tuple-element.18), channel_id=1, replica_groups={{130,131,192,193,194,195,256,257,258,259,320,321,322,323,384,385,386,38..., dimensions={0} | all-to-all | bytes 524288 | tf_op jit(solution)/shard_map/all_to_all | solution.py:214
  59.4 2.0 %shard_map.62 = (f32[144,128]{1,0:T(8,128)S(1)}, f32[4,128]{1,0:T(4,128)}) custom-call(bf16[512,48]{1,0:T(8,128)(2,1)S(1)} %get-tuple-element.16.x_ref, bf16[48,2048]{1,0:T(8,128)(2,1)S(1)} %get-tuple-element.13.y_ref, f32[1,128]{1,0:T(1,128)S(1)} %get-tuple-element.17.shift_ref, f32[32,16,128]{2,1,0:T(8,128)S(1)} %all_to_all.21.cols_ref), custom_call_target="tpu_custom_call" | custom-call | tf_op jit(solution)/shard_map/pallas_call | solution.py:219
  61.4 15.3 %all_to_all.22 = f32[16,9,1,128]{3,2,1,0:T(1,128)S(1)} all-to-all(f32[16,9,1,128]{3,2,1,0:T(1,128)S(1)} %bitcast.10), channel_id=1, replica_groups={{40,44,36,48,32,52,28,56,24,60,20,0,16,4,12,8},{41,45,37,49,33,53,29,57..., dimensions={0} | all-to-all | bytes 147456 | tf_op jit(solution)/shard_map/all_to_all | solution.py:214
  76.8 0.8 shard_map.63
  (1 shorter events, 0.0 us)
Async XLA Ops:
  0.6 0.7 copy-start.1
  2.1 17.5 %copy-start = (bf16[32,512]{1,0:T(8,128)(2,1)S(1)}, bf16[32,512]{1,0:T(8,128)(2,1)}, u32[]{:S(2)}) copy-start(bf16[32,512]{1,0:T(8,128)(2,1)} %samples_ref.1) | copy-start | bytes 98308
  2.1 17.5 %copy-start.2 = (f32[512]{0:T(512)S(1)}, f32[512]{0:T(512)}, u32[]{:S(2)}) copy-start(f32[512]{0:T(512)} %param.5) | copy-start | bytes 6148
  2.1 25.6 %all-to-all-start = ((bf16[16,8,128]{2,1,0:T(8,128)(2,1)}), bf16[16,8,128]{2,1,0:T(8,128)(2,1)S(1)}, u32[]{:S(2)}, u32[]{:S(2)}) async-start(bf16[16,8,128]{2,1,0:T(8,128)(2,1)} %shard_map.58), calls=%async_computation | async-start | bytes 65536 | tf_op jit(solution)/shard_map/all_to_all | solution.py:214

commit v7 on v6

--- a/solution.py
+++ b/solution.py
@@ -192,7 +192,7 @@
             second = jnp.where(lane[:, :, :128] == row[:, :, :128] + 8 * q, denom[:, q], second)
         second = jnp.sum(second, axis=1)
         for part in range(8):
-            peer = tile * 8 + part
+            peer = Z_PARTS.index(Z_ORDER[tile * 8 + part])
             parts_out[9 * peer : 9 * peer + 8, :] = first[part]
             parts_out[9 * peer + 8 : 9 * peer + 9, :128] = second[part : part + 1]
 
@@ -206,7 +206,9 @@
     bary_out[...] = turned(jnp.concatenate(stack, axis=0))[:32, :32] / denom[:, :32]
 
 
-Z_ORDER = (10, 11, 9, 12, 8, 13, 7, 14, 6, 15, 5, 0, 4, 1, 3, 2)
+Z_ORDER = (11, 12, 10, 13, 9, 14, 8, 15, 7, 0, 6, 1, 5, 2, 4, 3)
+Z_ROWS = (9, 10, 8, 11, 7, 12, 6, 13, 5, 14, 4, 15, 3, 0, 2, 1)
+Z_PARTS = (8, 9, 7, 10, 6, 11, 5, 12, 4, 13, 3, 14, 2, 15, 1, 0)
 PLANE_ORDER = (10, 11, 12, 13, 14, 15, 16, 17, 18, 19, 20, 21, 22, 23, 24, 25, 26, 27, 28, 29, 30, 31, 0, 1, 2, 3, 4, 5, 6, 7, 8, 9)
 
 
@@ -235,7 +237,7 @@
         [((POINTS, DEPTH), BF16), ((DEPTH, SAMPLES), BF16), ((16, 4, LANES), F32)],
         xs, ys,
     )
-    rows = exchange(rows, "z", Z_ORDER)
+    rows = exchange(rows, "z", Z_ROWS)
     x, shift, cols, point = call(
         col_pass,
         [((POINTS, DEPTH), BF16), ((1, LANES), F32), ((32, 16, LANES), F32), ((1, 32), F32)],
@@ -246,7 +248,7 @@
         weigh, [((144, LANES), F32), ((4, LANES), F32)], x, y, shift, cols
     )
     parts = parts.reshape(16, 9, 1, LANES)
-    parts = exchange(parts, "z", Z_ORDER).reshape(144, LANES)
+    parts = exchange(parts, "z", Z_PARTS).reshape(144, LANES)
     (bary,) = call(finish, [((32, 32), F32)], parts)
     return point.reshape(32), sample.reshape(512), bary
 

time: 78 us -> 76 us (0.974)
  blocking collectives: 52.8 us -> 51.8 us
  starting transfers between devices: 17.5 us -> 16.6 us
    all_to_all x3, blocking collectives: 44.7 us -> 43.7 us  [exchange(): return lax.all_to_all(value, axes, 0, 0, axis_index_groups=[list(order)])]
    all_to_all x1, starting transfers between devices: 17.5 us -> 16.6 us  [exchange(): return lax.all_to_all(value, axes, 0, 0, axis_index_groups=[list(order)])]
where the time goes in v7:
time: 76 us; the launch traced here: 75.6 us
  blocking collectives  51.8 us (68%)
  starting transfers between devices  16.6 us (22%)
  Pallas kernels  5.91 us (8%)
    all_to_all x3, blocking collectives, exchange(): return lax.all_to_all(value, axes, 0, 0, axis_index_groups=[list(order)])  43.7 us
    all_to_all x1, starting transfers between devices, exchange(): return lax.all_to_all(value, axes, 0, 0, axis_index_groups=[list(order)])  16.6 us
    all_gather x1, blocking collectives, on_device(): ys = lax.all_gather(own, ('x_hi', 'core'))  8.09 us
    pallas_call x6, Pallas kernels, call(): pl.pallas_call(body, out_shape=[jax.ShapeDtypeStruct(shape, dtype) for sh...  5.91 us
  transfers between devices with their start and end apart: 1, of which 0 were waited for; matrix products, arithmetic and copies ran while one was open for 0% of the time, Pallas kernels for 0%

profile of v7, /device:TPU:1, one launch (start us, length us, event | category | flops | bytes accessed | tf_op | source)
XLA Modules:
  0.0 75.6 jit_solution(1106148259076693533)
XLA Ops:
  0.6 0.0 copy-start.1
  0.6 0.7 copy-done.1
  1.3 0.7 shard_map.58
  2.1 0.0 copy-start
  2.1 0.0 copy-start.2
  2.1 16.6 %all-to-all-start = ((bf16[16,8,128]{2,1,0:T(8,128)(2,1)}), bf16[16,8,128]{2,1,0:T(8,128)(2,1)S(1)}, u32[]{:S(2)}, u32[]{:S(2)}) async-start(bf16[16,8,128]{2,1,0:T(8,128)(2,1)} %shard_map.58), calls=%async_computation | async-start | bytes 65536 | tf_op jit(solution)/shard_map/all_to_all | solution.py:216
  18.6 0.0 copy-done
  18.6 0.0 copy-done.2
  18.7 8.1 %all-gather = bf16[160,512]{1,0:T(8,128)(2,1)S(1)} all-gather(bf16[40,512]{1,0:T(8,128)(2,1)S(1)} %shard_map.59), channel_id=2, replica_groups=mesh['x_lo'=2,'y'=4,'z'=16,'x_hi'=2,'core'=2] {'x_hi','core'}, dimensions={0}, use_global_device_ids=true | all-gather | bytes 204800 | tf_op jit(solution)/shard_map/all_gather | solution.py:234
  26.8 0.0 all-to-all-done
  26.8 1.0 %shard_map.60 = (bf16[512,48]{1,0:T(8,128)(2,1)S(1)}, bf16[48,2048]{1,0:T(8,128)(2,1)S(1)}, f32[16,4,128]{2,1,0:T(4,128)S(1)}) custom-call(bf16[128,128]{1,0:T(8,128)(2,1)S(1)} %bitcast.9, bf16[4,40,512]{2,1,0:T(8,128)(2,1)S(1)} %bitcast.7), custom_call_target="tpu_custom_call" | custom-call | tf_op jit(solution)/shard_map/pallas_call | solution.py:221
  27.8 14.6 %all_to_all.20.rows_ref = f32[16,4,128]{2,1,0:T(4,128)S(1)} all-to-all(f32[16,4,128]{2,1,0:T(4,128)S(1)} %get-tuple-element.14), channel_id=1, replica_groups={{36,40,32,44,28,48,24,52,20,56,16,60,12,0,8,4},{37,41,33,45,29,49,25,53..., dimensions={0} | all-to-all | bytes 65536 | tf_op jit(solution)/shard_map/all_to_all | solution.py:216
  42.4 1.4 %shard_map.61 = (bf16[512,48]{1,0:T(8,128)(2,1)S(1)}, f32[1,128]{1,0:T(1,128)S(1)}, f32[32,16,128]{2,1,0:T(8,128)S(1)}, f32[1,32]{1,0:T(1,128)}) custom-call(bf16[512,48]{1,0:T(8,128)(2,1)S(1)} %get-tuple-element.12.x_ref, bf16[48,2048]{1,0:T(8,128)(2,1)S(1)} %get-tuple-element.13.y_ref, f32[16,4,128]{2,1,0:T(4,128)S(1)} %all_to_all.20.rows_ref), custom_call_target="tpu_custom_call" | custom-call | tf_op jit(solution)/shard_map/pallas_call | solution.py:221
  43.8 13.9 %all_to_all.21.cols_ref = f32[32,16,128]{2,1,0:T(8,128)S(1)} all-to-all(f32[32,16,128]{2,1,0:T(8,128)S(1)} %get-tuple-element.18), channel_id=1, replica_groups={{130,131,192,193,194,195,256,257,258,259,320,321,322,323,384,385,386,38..., dimensions={0} | all-to-all | bytes 524288 | tf_op jit(solution)/shard_map/all_to_all | solution.py:216
  57.6 2.0 %shard_map.62 = (f32[144,128]{1,0:T(8,128)S(1)}, f32[4,128]{1,0:T(4,128)}) custom-call(bf16[512,48]{1,0:T(8,128)(2,1)S(1)} %get-tuple-element.16.x_ref, bf16[48,2048]{1,0:T(8,128)(2,1)S(1)} %get-tuple-element.13.y_ref, f32[1,128]{1,0:T(1,128)S(1)} %get-tuple-element.17.shift_ref, f32[32,16,128]{2,1,0:T(8,128)S(1)} %all_to_all.21.cols_ref), custom_call_target="tpu_custom_call" | custom-call | tf_op jit(solution)/shard_map/pallas_call | solution.py:221
  59.6 15.2 %all_to_all.22 = f32[16,9,1,128]{3,2,1,0:T(1,128)S(1)} all-to-all(f32[16,9,1,128]{3,2,1,0:T(1,128)S(1)} %bitcast.10), channel_id=1, replica_groups={{32,36,28,40,24,44,20,48,16,52,12,56,8,60,4,0},{33,37,29,41,25,45,21,49..., dimensions={0} | all-to-all | bytes 147456 | tf_op jit(solution)/shard_map/all_to_all | solution.py:216
  74.8 0.8 %shard_map.63 = f32[32,32]{1,0:T(8,128)} custom-call(f32[144,128]{1,0:T(8,128)S(1)} %bitcast.8), custom_call_target="tpu_custom_call" | custom-call | tf_op jit(solution)/shard_map/pallas_call | solution.py:221
  (1 shorter events, 0.0 us)
Async XLA Ops:
  0.6 0.7 copy-start.1
  2.1 16.6 %copy-start = (bf16[32,512]{1,0:T(8,128)(2,1)S(1)}, bf16[32,512]{1,0:T(8,128)(2,1)}, u32[]{:S(2)}) copy-start(bf16[32,512]{1,0:T(8,128)(2,1)} %samples_ref.1) | copy-start | bytes 98308
  2.1 16.6 %copy-start.2 = (f32[512]{0:T(512)S(1)}, f32[512]{0:T(512)}, u32[]{:S(2)}) copy-start(f32[512]{0:T(512)} %param.5) | copy-start | bytes 6148
  2.1 24.7 %all-to-all-start = ((bf16[16,8,128]{2,1,0:T(8,128)(2,1)}), bf16[16,8,128]{2,1,0:T(8,128)(2,1)S(1)}, u32[]{:S(2)}, u32[]{:S(2)}) async-start(bf16[16,8,128]{2,1,0:T(8,128)(2,1)} %shard_map.58), calls=%async_computation | async-start | bytes 65536 | tf_op jit(solution)/shard_map/all_to_all | solution.py:216

commit v8 on v7

--- a/solution.py
+++ b/solution.py
@@ -129,7 +129,7 @@
     lse_out[...] = jnp.broadcast_to(stack_up(lines)[None], (16, 4, LANES))
 
 
-def col_pass(x_ref, y_ref, rows_ref, x_out, shift_out, lse_out, own_out):
+def col_pass(x_ref, y_ref, rows_ref, x_out, shift_out, sums_out, own_out):
     point = (LOG_SAMPLES - combine(rows_ref[...])) / SCALE
     z = lax.axis_index("z")
     z = sum(jnp.where(z == other, slot, 0) for slot, other in enumerate(Z_ORDER))
@@ -156,13 +156,22 @@
             left = x[tile * 128 : tile * 128 + 128]
             part = jnp.exp2(jnp.dot(left, right, preferred_element_type=F32) * SCALE)
             total += jnp.sum(part.reshape(16, 8, 256), axis=0)
-        total = jnp.log2(jnp.sum(total, axis=0, keepdims=True)) + SCALE * shift
+        total = jnp.sum(total, axis=0, keepdims=True)
         lines += [total[:, :LANES], total[:, LANES:]]
-    lse_out[...] = jnp.broadcast_to(stack_up(lines)[None], (32, 16, LANES))
+    lane = lanes_of((8, LANES))
+    block = jnp.zeros((8, LANES), F32)
+    for k, part in enumerate(triple(jnp.full((1, LANES), shift, F32))):
+        block = jnp.where(lane == k, part, block)
+    block = jnp.concatenate([stack_up(lines), block], axis=0).astype(BF16)
+    sums_out[...] = jnp.broadcast_to(block[None], (32, 24, LANES))
 
 
 def weigh(x_ref, y_ref, shift_ref, cols_ref, parts_out, sample_out):
-    sample = (LOG_POINTS - combine(cols_ref[...])) / SCALE
+    cols = cols_ref[...].astype(F32)
+    moved = jnp.sum(cols[:, 16:], axis=(1, 2), keepdims=True) / 8
+    most = jnp.max(moved)
+    total = jnp.sum(cols[:, :16] * jnp.exp2((moved - most) * SCALE), axis=0)
+    sample = (LOG_POINTS - jnp.log2(total)) / SCALE - most
     side = lax.axis_index("x_hi") * 2 + lax.axis_index("core")
     own = sample[:4]
     for k in range(1, 4):
@@ -240,7 +249,7 @@
     rows = exchange(rows, "z", Z_ROWS)
     x, shift, cols, point = call(
         col_pass,
-        [((POINTS, DEPTH), BF16), ((1, LANES), F32), ((32, 16, LANES), F32), ((1, 32), F32)],
+        [((POINTS, DEPTH), BF16), ((1, LANES), F32), ((32, 24, LANES), BF16), ((1, 32), F32)],
         x, y, rows,
     )
     cols = exchange(cols, PLANE, PLANE_ORDER)

time: 76 us -> 75.2 us (0.989)
  no operation moved by 1% of the time
where the time goes in v8:
time: 75.2 us; the launch traced here: 74.9 us
  blocking collectives  51.1 us (68%)
  starting transfers between devices  16.6 us (22%)
  Pallas kernels  5.81 us (8%)
    all_to_all x3, blocking collectives, exchange(): return lax.all_to_all(value, axes, 0, 0, axis_index_groups=[list(order)])  43 us
    all_to_all x1, starting transfers between devices, exchange(): return lax.all_to_all(value, axes, 0, 0, axis_index_groups=[list(order)])  16.6 us
    all_gather x1, blocking collectives, on_device(): ys = lax.all_gather(own, ('x_hi', 'core'))  8.09 us
    pallas_call x6, Pallas kernels, call(): pl.pallas_call(body, out_shape=[jax.ShapeDtypeStruct(shape, dtype) for sh...  5.81 us
  transfers between devices with their start and end apart: 1, of which 0 were waited for; matrix products, arithmetic and copies ran while one was open for 0% of the time, Pallas kernels for 0%

profile of v8, /device:TPU:1, one launch (start us, length us, event | category | flops | bytes accessed | tf_op | source)
XLA Modules:
  0.0 74.9 jit_solution(6396710244071594360)
XLA Ops:
  0.6 0.0 copy-start.1
  0.6 0.7 copy-done.1
  1.3 0.7 shard_map.58
  2.1 0.0 copy-start
  2.1 0.0 copy-start.2
  2.1 16.6 %all-to-all-start = ((bf16[16,8,128]{2,1,0:T(8,128)(2,1)}), bf16[16,8,128]{2,1,0:T(8,128)(2,1)S(1)}, u32[]{:S(2)}, u32[]{:S(2)}) async-start(bf16[16,8,128]{2,1,0:T(8,128)(2,1)} %shard_map.58), calls=%async_computation | async-start | bytes 65536 | tf_op jit(solution)/shard_map/all_to_all | solution.py:225
  18.6 0.0 copy-done
  18.6 0.0 copy-done.2
  18.7 8.1 %all-gather = bf16[160,512]{1,0:T(8,128)(2,1)S(1)} all-gather(bf16[40,512]{1,0:T(8,128)(2,1)S(1)} %shard_map.59), channel_id=2, replica_groups=mesh['x_lo'=2,'y'=4,'z'=16,'x_hi'=2,'core'=2] {'x_hi','core'}, dimensions={0}, use_global_device_ids=true | all-gather | bytes 204800 | tf_op jit(solution)/shard_map/all_gather | solution.py:243
  26.8 0.0 all-to-all-done
  26.8 1.0 %shard_map.60 = (bf16[512,48]{1,0:T(8,128)(2,1)S(1)}, bf16[48,2048]{1,0:T(8,128)(2,1)S(1)}, f32[16,4,128]{2,1,0:T(4,128)S(1)}) custom-call(bf16[128,128]{1,0:T(8,128)(2,1)S(1)} %bitcast.9, bf16[4,40,512]{2,1,0:T(8,128)(2,1)S(1)} %bitcast.7), custom_call_target="tpu_custom_call" | custom-call | tf_op jit(solution)/shard_map/pallas_call | solution.py:230
  27.8 14.6 %all_to_all.20.rows_ref = f32[16,4,128]{2,1,0:T(4,128)S(1)} all-to-all(f32[16,4,128]{2,1,0:T(4,128)S(1)} %get-tuple-element.14), channel_id=1, replica_groups={{36,40,32,44,28,48,24,52,20,56,16,60,12,0,8,4},{37,41,33,45,29,49,25,53..., dimensions={0} | all-to-all | bytes 65536 | tf_op jit(solution)/shard_map/all_to_all | solution.py:225
  42.4 1.4 %shard_map.61 = (bf16[512,48]{1,0:T(8,128)(2,1)S(1)}, f32[1,128]{1,0:T(1,128)S(1)}, bf16[32,24,128]{2,1,0:T(8,128)(2,1)S(1)}, f32[1,32]{1,0:T(1,128)}) custom-call(bf16[512,48]{1,0:T(8,128)(2,1)S(1)} %get-tuple-element.12.x_ref, bf16[48,2048]{1,0:T(8,128)(2,1)S(1)} %get-tuple-element.13.y_ref, f32[16,4,128]{2,1,0:T(4,128)S(1)} %all_to_all.20.rows_ref), custom_call_target="tpu_custom_call" | custom-call | tf_op jit(solution)/shard_map/pallas_call | solution.py:230
  43.8 13.2 %all_to_all.21.cols_ref = bf16[32,24,128]{2,1,0:T(8,128)(2,1)S(1)} all-to-all(bf16[32,24,128]{2,1,0:T(8,128)(2,1)S(1)} %get-tuple-element.18), channel_id=1, replica_groups={{130,131,192,193,194,195,256,257,258,259,320,321,322,323,384,385,386,38..., dimensions={0} | all-to-all | bytes 393216 | tf_op jit(solution)/shard_map/all_to_all | solution.py:225
  57.0 1.9 %shard_map.62 = (f32[144,128]{1,0:T(8,128)S(1)}, f32[4,128]{1,0:T(4,128)}) custom-call(bf16[512,48]{1,0:T(8,128)(2,1)S(1)} %get-tuple-element.16.x_ref, bf16[48,2048]{1,0:T(8,128)(2,1)S(1)} %get-tuple-element.13.y_ref, f32[1,128]{1,0:T(1,128)S(1)} %get-tuple-element.17.shift_ref, bf16[32,24,128]{2,1,0:T(8,128)(2,1)S(1)} %all_to_all.21.cols_ref), custom_call_target="tpu_custom_call" | custom-call | tf_op jit(solution)/shard_map/pallas_call | solution.py:230
  58.9 15.2 %all_to_all.22 = f32[16,9,1,128]{3,2,1,0:T(1,128)S(1)} all-to-all(f32[16,9,1,128]{3,2,1,0:T(1,128)S(1)} %bitcast.10), channel_id=1, replica_groups={{32,36,28,40,24,44,20,48,16,52,12,56,8,60,4,0},{33,37,29,41,25,45,21,49..., dimensions={0} | all-to-all | bytes 147456 | tf_op jit(solution)/shard_map/all_to_all | solution.py:225
  74.1 0.8 %shard_map.63 = f32[32,32]{1,0:T(8,128)} custom-call(f32[144,128]{1,0:T(8,128)S(1)} %bitcast.8), custom_call_target="tpu_custom_call" | custom-call | tf_op jit(solution)/shard_map/pallas_call | solution.py:230
  (1 shorter events, 0.0 us)
Async XLA Ops:
  0.6 0.7 copy-start.1
  2.1 16.6 %copy-start = (bf16[32,512]{1,0:T(8,128)(2,1)S(1)}, bf16[32,512]{1,0:T(8,128)(2,1)}, u32[]{:S(2)}) copy-start(bf16[32,512]{1,0:T(8,128)(2,1)} %samples_ref.1) | copy-start | bytes 98308
  2.1 16.6 %copy-start.2 = (f32[512]{0:T(512)S(1)}, f32[512]{0:T(512)}, u32[]{:S(2)}) copy-start(f32[512]{0:T(512)} %param.5) | copy-start | bytes 6148
  2.1 24.7 %all-to-all-start = ((bf16[16,8,128]{2,1,0:T(8,128)(2,1)}), bf16[16,8,128]{2,1,0:T(8,128)(2,1)S(1)}, u32[]{:S(2)}, u32[]{:S(2)}) async-start(bf16[16,8,128]{2,1,0:T(8,128)(2,1)} %shard_map.58), calls=%async_computation | async-start | bytes 65536 | tf_op jit(solution)/shard_map/all_to_all | solution.py:225

commit v9 on v8

--- a/solution.py
+++ b/solution.py
@@ -215,7 +215,7 @@
     bary_out[...] = turned(jnp.concatenate(stack, axis=0))[:32, :32] / denom[:, :32]
 
 
-Z_ORDER = (11, 12, 10, 13, 9, 14, 8, 15, 7, 0, 6, 1, 5, 2, 4, 3)
+Z_ORDER = (12, 13, 11, 14, 10, 15, 9, 0, 8, 1, 7, 2, 6, 3, 5, 4)
 Z_ROWS = (9, 10, 8, 11, 7, 12, 6, 13, 5, 14, 4, 15, 3, 0, 2, 1)
 Z_PARTS = (8, 9, 7, 10, 6, 11, 5, 12, 4, 13, 3, 14, 2, 15, 1, 0)
 PLANE_ORDER = (10, 11, 12, 13, 14, 15, 16, 17, 18, 19, 20, 21, 22, 23, 24, 25, 26, 27, 28, 29, 30, 31, 0, 1, 2, 3, 4, 5, 6, 7, 8, 9)
@@ -240,7 +240,8 @@
     (xs,) = call(prepare_points, [((16, 8, LANES), BF16)], points)
     xs = exchange(xs, "z", Z_ORDER).reshape(LANES, LANES)
     (own,) = call(prepare_samples, [((40, 512), BF16)], samples, potential.reshape(1, 512))
-    ys = lax.all_gather(own, ("x_hi", "core"))
+    near = [[0, 1, 6, 7], [4, 5, 2, 3]]
+    ys = lax.all_gather(own, ("x_lo", "x_hi", "core"), axis_index_groups=near)
     x, y, rows = call(
         row_pass,
         [((POINTS, DEPTH), BF16), ((DEPTH, SAMPLES), BF16), ((16, 4, LANES), F32)],

time: 75.2 us -> 74.6 us (level)
  no operation moved by 1% of the time
where the time goes in v9:
time: 74.6 us; the launch traced here: 74.2 us
  blocking collectives  50.9 us (68%)
  starting transfers between devices  16.1 us (22%)
  Pallas kernels  5.82 us (8%)
    all_to_all x3, blocking collectives, exchange(): return lax.all_to_all(value, axes, 0, 0, axis_index_groups=[list(order)])  43.1 us
    all_to_all x1, starting transfers between devices, exchange(): return lax.all_to_all(value, axes, 0, 0, axis_index_groups=[list(order)])  16.1 us
    all_gather x1, blocking collectives, on_device(): ys = lax.all_gather(own, ('x_lo', 'x_hi', 'core'), axis_index_groups=near)  7.8 us
    pallas_call x6, Pallas kernels, call(): pl.pallas_call(body, out_shape=[jax.ShapeDtypeStruct(shape, dtype) for sh...  5.82 us
  transfers between devices with their start and end apart: 1, of which 0 were waited for; matrix products, arithmetic and copies ran while one was open for 0% of the time, Pallas kernels for 0%

profile of v9, /device:TPU:1, one launch (start us, length us, event | category | flops | bytes accessed | tf_op | source)
XLA Modules:
  0.0 74.2 jit_solution(5484250298031973544)
XLA Ops:
  0.6 0.0 copy-start.1
  0.6 0.7 copy-done.1
  1.3 0.7 %shard_map.58 = bf16[16,8,128]{2,1,0:T(8,128)(2,1)} custom-call(bf16[32,32]{1,0:T(8,128)(2,1)S(1)} %copy-done.1), custom_call_target="tpu_custom_call" | custom-call | tf_op jit(solution)/shard_map/pallas_call | solution.py:230
  2.1 0.0 copy-start
  2.1 0.0 copy-start.2
  2.1 16.1 %all-to-all-start = ((bf16[16,8,128]{2,1,0:T(8,128)(2,1)}), bf16[16,8,128]{2,1,0:T(8,128)(2,1)S(1)}, u32[]{:S(2)}, u32[]{:S(2)}) async-start(bf16[16,8,128]{2,1,0:T(8,128)(2,1)} %shard_map.58), calls=%async_computation | async-start | bytes 65536 | tf_op jit(solution)/shard_map/all_to_all | solution.py:225
  18.1 0.0 copy-done
  18.2 0.0 copy-done.2
  18.2 7.8 %all-gather = bf16[160,512]{1,0:T(8,128)(2,1)S(1)} all-gather(bf16[40,512]{1,0:T(8,128)(2,1)S(1)} %shard_map.59), channel_id=2, replica_groups={{0,1,258,259},{256,257,2,3},{4,5,262,263},{260,261,6,7},{8,9,266,267},{..., dimensions={0}, use_global_device_ids=true | all-gather | bytes 204800 | tf_op jit(solution)/shard_map/all_gather | solution.py:244
  26.0 0.0 all-to-all-done
  26.0 1.0 %shard_map.60 = (bf16[512,48]{1,0:T(8,128)(2,1)S(1)}, bf16[48,2048]{1,0:T(8,128)(2,1)S(1)}, f32[16,4,128]{2,1,0:T(4,128)S(1)}) custom-call(bf16[128,128]{1,0:T(8,128)(2,1)S(1)} %bitcast.9, bf16[4,40,512]{2,1,0:T(8,128)(2,1)S(1)} %bitcast.7), custom_call_target="tpu_custom_call" | custom-call | tf_op jit(solution)/shard_map/pallas_call | solution.py:230
  27.0 14.6 %all_to_all.20.rows_ref = f32[16,4,128]{2,1,0:T(4,128)S(1)} all-to-all(f32[16,4,128]{2,1,0:T(4,128)S(1)} %get-tuple-element.14), channel_id=1, replica_groups={{36,40,32,44,28,48,24,52,20,56,16,60,12,0,8,4},{37,41,33,45,29,49,25,53..., dimensions={0} | all-to-all | bytes 65536 | tf_op jit(solution)/shard_map/all_to_all | solution.py:225
  41.6 1.4 %shard_map.61 = (bf16[512,48]{1,0:T(8,128)(2,1)S(1)}, f32[1,128]{1,0:T(1,128)S(1)}, bf16[32,24,128]{2,1,0:T(8,128)(2,1)S(1)}, f32[1,32]{1,0:T(1,128)}) custom-call(bf16[512,48]{1,0:T(8,128)(2,1)S(1)} %get-tuple-element.12.x_ref, bf16[48,2048]{1,0:T(8,128)(2,1)S(1)} %get-tuple-element.13.y_ref, f32[16,4,128]{2,1,0:T(4,128)S(1)} %all_to_all.20.rows_ref), custom_call_target="tpu_custom_call" | custom-call | tf_op jit(solution)/shard_map/pallas_call | solution.py:230
  43.0 13.3 %all_to_all.21.cols_ref = bf16[32,24,128]{2,1,0:T(8,128)(2,1)S(1)} all-to-all(bf16[32,24,128]{2,1,0:T(8,128)(2,1)S(1)} %get-tuple-element.18), channel_id=1, replica_groups={{130,131,192,193,194,195,256,257,258,259,320,321,322,323,384,385,386,38..., dimensions={0} | all-to-all | bytes 393216 | tf_op jit(solution)/shard_map/all_to_all | solution.py:225
  56.3 1.9 %shard_map.62 = (f32[144,128]{1,0:T(8,128)S(1)}, f32[4,128]{1,0:T(4,128)}) custom-call(bf16[512,48]{1,0:T(8,128)(2,1)S(1)} %get-tuple-element.16.x_ref, bf16[48,2048]{1,0:T(8,128)(2,1)S(1)} %get-tuple-element.13.y_ref, f32[1,128]{1,0:T(1,128)S(1)} %get-tuple-element.17.shift_ref, bf16[32,24,128]{2,1,0:T(8,128)(2,1)S(1)} %all_to_all.21.cols_ref), custom_call_target="tpu_custom_call" | custom-call | tf_op jit(solution)/shard_map/pallas_call | solution.py:230
  58.2 15.2 %all_to_all.22 = f32[16,9,1,128]{3,2,1,0:T(1,128)S(1)} all-to-all(f32[16,9,1,128]{3,2,1,0:T(1,128)S(1)} %bitcast.10), channel_id=1, replica_groups={{32,36,28,40,24,44,20,48,16,52,12,56,8,60,4,0},{33,37,29,41,25,45,21,49..., dimensions={0} | all-to-all | bytes 147456 | tf_op jit(solution)/shard_map/all_to_all | solution.py:225
  73.4 0.8 %shard_map.63 = f32[32,32]{1,0:T(8,128)} custom-call(f32[144,128]{1,0:T(8,128)S(1)} %bitcast.8), custom_call_target="tpu_custom_call" | custom-call | tf_op jit(solution)/shard_map/pallas_call | solution.py:230
  (1 shorter events, 0.0 us)
Async XLA Ops:
  0.6 0.7 copy-start.1
  2.1 16.1 %copy-start = (bf16[32,512]{1,0:T(8,128)(2,1)S(1)}, bf16[32,512]{1,0:T(8,128)(2,1)}, u32[]{:S(2)}) copy-start(bf16[32,512]{1,0:T(8,128)(2,1)} %samples_ref.1) | copy-start | bytes 98308
  2.1 16.1 %copy-start.2 = (f32[512]{0:T(512)S(1)}, f32[512]{0:T(512)}, u32[]{:S(2)}) copy-start(f32[512]{0:T(512)} %param.5) | copy-start | bytes 6148
  2.1 23.9 %all-to-all-start = ((bf16[16,8,128]{2,1,0:T(8,128)(2,1)}), bf16[16,8,128]{2,1,0:T(8,128)(2,1)S(1)}, u32[]{:S(2)}, u32[]{:S(2)}) async-start(bf16[16,8,128]{2,1,0:T(8,128)(2,1)} %shard_map.58), calls=%async_computation | async-start | bytes 65536 | tf_op jit(solution)/shard_map/all_to_all | solution.py:225

commit v10 on v9

--- a/solution.py
+++ b/solution.py
@@ -218,7 +218,7 @@
 Z_ORDER = (12, 13, 11, 14, 10, 15, 9, 0, 8, 1, 7, 2, 6, 3, 5, 4)
 Z_ROWS = (9, 10, 8, 11, 7, 12, 6, 13, 5, 14, 4, 15, 3, 0, 2, 1)
 Z_PARTS = (8, 9, 7, 10, 6, 11, 5, 12, 4, 13, 3, 14, 2, 15, 1, 0)
-PLANE_ORDER = (10, 11, 12, 13, 14, 15, 16, 17, 18, 19, 20, 21, 22, 23, 24, 25, 26, 27, 28, 29, 30, 31, 0, 1, 2, 3, 4, 5, 6, 7, 8, 9)
+PLANE_ORDER = (10, 11, 6, 14, 24, 26, 7, 15, 25, 27, 2, 8, 20, 22, 28, 30, 3, 9, 21, 23, 29, 31, 4, 12, 16, 18, 5, 13, 17, 19, 0, 1)
 
 
 def exchange(value, axes, order):

time: 74.6 us -> 74.2 us (level)
    all_to_all x3, blocking collectives: 43.1 us -> 42.4 us  [exchange(): return lax.all_to_all(value, axes, 0, 0, axis_index_groups=[list(order)])]
where the time goes in v10:
time: 74.2 us; the launch traced here: 73.4 us
  blocking collectives  50.2 us (68%)
  starting transfers between devices  16.1 us (22%)
  Pallas kernels  5.82 us (8%)
    all_to_all x3, blocking collectives, exchange(): return lax.all_to_all(value, axes, 0, 0, axis_index_groups=[list(order)])  42.4 us
    all_to_all x1, starting transfers between devices, exchange(): return lax.all_to_all(value, axes, 0, 0, axis_index_groups=[list(order)])  16.1 us
    all_gather x1, blocking collectives, on_device(): ys = lax.all_gather(own, ('x_lo', 'x_hi', 'core'), axis_index_groups=near)  7.8 us
    pallas_call x6, Pallas kernels, call(): pl.pallas_call(body, out_shape=[jax.ShapeDtypeStruct(shape, dtype) for sh...  5.82 us
  transfers between devices with their start and end apart: 1, of which 0 were waited for; matrix products, arithmetic and copies ran while one was open for 0% of the time, Pallas kernels for 0%

profile of v10, /device:TPU:1, one launch (start us, length us, event | category | flops | bytes accessed | tf_op | source)
XLA Modules:
  0.0 73.4 jit_solution(13388694503320673464)
XLA Ops:
  0.6 0.0 copy-start.1
  0.6 0.7 copy-done.1
  1.3 0.7 %shard_map.58 = bf16[16,8,128]{2,1,0:T(8,128)(2,1)} custom-call(bf16[32,32]{1,0:T(8,128)(2,1)S(1)} %copy-done.1), custom_call_target="tpu_custom_call" | custom-call | tf_op jit(solution)/shard_map/pallas_call | solution.py:230
  2.1 0.0 copy-start
  2.1 0.0 copy-start.2
  2.1 16.1 %all-to-all-start = ((bf16[16,8,128]{2,1,0:T(8,128)(2,1)}), bf16[16,8,128]{2,1,0:T(8,128)(2,1)S(1)}, u32[]{:S(2)}, u32[]{:S(2)}) async-start(bf16[16,8,128]{2,1,0:T(8,128)(2,1)} %shard_map.58), calls=%async_computation | async-start | bytes 65536 | tf_op jit(solution)/shard_map/all_to_all | solution.py:225
  18.1 0.0 copy-done
  18.2 0.0 copy-done.2
  18.2 7.8 %all-gather = bf16[160,512]{1,0:T(8,128)(2,1)S(1)} all-gather(bf16[40,512]{1,0:T(8,128)(2,1)S(1)} %shard_map.59), channel_id=2, replica_groups={{0,1,258,259},{256,257,2,3},{4,5,262,263},{260,261,6,7},{8,9,266,267},{..., dimensions={0}, use_global_device_ids=true | all-gather | bytes 204800 | tf_op jit(solution)/shard_map/all_gather | solution.py:244
  26.0 0.0 all-to-all-done
  26.0 1.0 %shard_map.60 = (bf16[512,48]{1,0:T(8,128)(2,1)S(1)}, bf16[48,2048]{1,0:T(8,128)(2,1)S(1)}, f32[16,4,128]{2,1,0:T(4,128)S(1)}) custom-call(bf16[128,128]{1,0:T(8,128)(2,1)S(1)} %bitcast.9, bf16[4,40,512]{2,1,0:T(8,128)(2,1)S(1)} %bitcast.7), custom_call_target="tpu_custom_call" | custom-call | tf_op jit(solution)/shard_map/pallas_call | solution.py:230
  27.0 14.6 %all_to_all.20.rows_ref = f32[16,4,128]{2,1,0:T(4,128)S(1)} all-to-all(f32[16,4,128]{2,1,0:T(4,128)S(1)} %get-tuple-element.14), channel_id=1, replica_groups={{36,40,32,44,28,48,24,52,20,56,16,60,12,0,8,4},{37,41,33,45,29,49,25,53..., dimensions={0} | all-to-all | bytes 65536 | tf_op jit(solution)/shard_map/all_to_all | solution.py:225
  41.6 1.4 %shard_map.61 = (bf16[512,48]{1,0:T(8,128)(2,1)S(1)}, f32[1,128]{1,0:T(1,128)S(1)}, bf16[32,24,128]{2,1,0:T(8,128)(2,1)S(1)}, f32[1,32]{1,0:T(1,128)}) custom-call(bf16[512,48]{1,0:T(8,128)(2,1)S(1)} %get-tuple-element.12.x_ref, bf16[48,2048]{1,0:T(8,128)(2,1)S(1)} %get-tuple-element.13.y_ref, f32[16,4,128]{2,1,0:T(4,128)S(1)} %all_to_all.20.rows_ref), custom_call_target="tpu_custom_call" | custom-call | tf_op jit(solution)/shard_map/pallas_call | solution.py:230
  43.0 13.2 %all_to_all.21.cols_ref = bf16[32,24,128]{2,1,0:T(8,128)(2,1)S(1)} all-to-all(bf16[32,24,128]{2,1,0:T(8,128)(2,1)S(1)} %get-tuple-element.18), channel_id=1, replica_groups={{130,131,66,194,384,386,67,195,385,387,2,128,320,322,448,450,3,129,321,..., dimensions={0} | all-to-all | bytes 393216 | tf_op jit(solution)/shard_map/all_to_all | solution.py:225
  56.2 1.9 %shard_map.62 = (f32[144,128]{1,0:T(8,128)S(1)}, f32[4,128]{1,0:T(4,128)}) custom-call(bf16[512,48]{1,0:T(8,128)(2,1)S(1)} %get-tuple-element.16.x_ref, bf16[48,2048]{1,0:T(8,128)(2,1)S(1)} %get-tuple-element.13.y_ref, f32[1,128]{1,0:T(1,128)S(1)} %get-tuple-element.17.shift_ref, bf16[32,24,128]{2,1,0:T(8,128)(2,1)S(1)} %all_to_all.21.cols_ref), custom_call_target="tpu_custom_call" | custom-call | tf_op jit(solution)/shard_map/pallas_call | solution.py:230
  58.1 14.5 %all_to_all.22 = f32[16,9,1,128]{3,2,1,0:T(1,128)S(1)} all-to-all(f32[16,9,1,128]{3,2,1,0:T(1,128)S(1)} %bitcast.10), channel_id=1, replica_groups={{32,36,28,40,24,44,20,48,16,52,12,56,8,60,4,0},{33,37,29,41,25,45,21,49..., dimensions={0} | all-to-all | bytes 147456 | tf_op jit(solution)/shard_map/all_to_all | solution.py:225
  72.6 0.8 %shard_map.63 = f32[32,32]{1,0:T(8,128)} custom-call(f32[144,128]{1,0:T(8,128)S(1)} %bitcast.8), custom_call_target="tpu_custom_call" | custom-call | tf_op jit(solution)/shard_map/pallas_call | solution.py:230
  (1 shorter events, 0.0 us)
Async XLA Ops:
  0.6 0.7 copy-start.1
  2.1 16.1 %copy-start = (bf16[32,512]{1,0:T(8,128)(2,1)S(1)}, bf16[32,512]{1,0:T(8,128)(2,1)}, u32[]{:S(2)}) copy-start(bf16[32,512]{1,0:T(8,128)(2,1)} %samples_ref.1) | copy-start | bytes 98308
  2.1 16.1 %copy-start.2 = (f32[512]{0:T(512)S(1)}, f32[512]{0:T(512)}, u32[]{:S(2)}) copy-start(f32[512]{0:T(512)} %param.5) | copy-start | bytes 6148
  2.1 23.9 %all-to-all-start = ((bf16[16,8,128]{2,1,0:T(8,128)(2,1)}), bf16[16,8,128]{2,1,0:T(8,128)(2,1)S(1)}, u32[]{:S(2)}, u32[]{:S(2)}) async-start(bf16[16,8,128]{2,1,0:T(8,128)(2,1)} %shard_map.58), calls=%async_computation | async-start | bytes 65536 | tf_op jit(solution)/shard_map/all_to_all | solution.py:225

commit v11 on v10

--- a/solution.py
+++ b/solution.py
@@ -107,7 +107,7 @@
         x = jnp.where(lane == 35 + k, part, x)
     x = x[:, :DEPTH].astype(BF16)
     x_out[...] = x
-    y = jnp.concatenate([samples_ref[k].astype(F32) for k in range(4)], axis=1)
+    y = jnp.concatenate([samples_ref[k].astype(F32) for k in (2, 3, 0, 1)], axis=1)
     pot = jnp.sum(y[32:40], axis=0, keepdims=True)
     y = y[:32]
     y_norm = -0.5 * jnp.sum(y * y, axis=0, keepdims=True)
@@ -240,7 +240,7 @@
     (xs,) = call(prepare_points, [((16, 8, LANES), BF16)], points)
     xs = exchange(xs, "z", Z_ORDER).reshape(LANES, LANES)
     (own,) = call(prepare_samples, [((40, 512), BF16)], samples, potential.reshape(1, 512))
-    near = [[0, 1, 6, 7], [4, 5, 2, 3]]
+    near = [[6, 7, 0, 1], [2, 3, 4, 5]]
     ys = lax.all_gather(own, ("x_lo", "x_hi", "core"), axis_index_groups=near)
     x, y, rows = call(
         row_pass,

time: 74.2 us -> 74.2 us (level)
  no operation moved by 1% of the time
where the time goes in v11:
time: 74.2 us; the launch traced here: 73.4 us
  blocking collectives  50.2 us (68%)
  starting transfers between devices  16.1 us (22%)
  Pallas kernels  5.82 us (8%)
    all_to_all x3, blocking collectives, exchange(): return lax.all_to_all(value, axes, 0, 0, axis_index_groups=[list(order)])  42.4 us
    all_to_all x1, starting transfers between devices, exchange(): return lax.all_to_all(value, axes, 0, 0, axis_index_groups=[list(order)])  16.1 us
    all_gather x1, blocking collectives, on_device(): ys = lax.all_gather(own, ('x_lo', 'x_hi', 'core'), axis_index_groups=near)  7.8 us
    pallas_call x6, Pallas kernels, call(): pl.pallas_call(body, out_shape=[jax.ShapeDtypeStruct(shape, dtype) for sh...  5.82 us
  transfers between devices with their start and end apart: 1, of which 0 were waited for; matrix products, arithmetic and copies ran while one was open for 0% of the time, Pallas kernels for 0%

profile of v11, /device:TPU:1, one launch (start us, length us, event | category | flops | bytes accessed | tf_op | source)
XLA Modules:
  0.0 73.4 jit_solution(3652192689018083315)
XLA Ops:
  0.6 0.0 copy-start.1
  0.6 0.7 copy-done.1
  1.3 0.7 %shard_map.58 = bf16[16,8,128]{2,1,0:T(8,128)(2,1)} custom-call(bf16[32,32]{1,0:T(8,128)(2,1)S(1)} %copy-done.1), custom_call_target="tpu_custom_call" | custom-call | tf_op jit(solution)/shard_map/pallas_call | solution.py:230
  2.1 0.0 copy-start
  2.1 0.0 copy-start.2
  2.1 16.1 %all-to-all-start = ((bf16[16,8,128]{2,1,0:T(8,128)(2,1)}), bf16[16,8,128]{2,1,0:T(8,128)(2,1)S(1)}, u32[]{:S(2)}, u32[]{:S(2)}) async-start(bf16[16,8,128]{2,1,0:T(8,128)(2,1)} %shard_map.58), calls=%async_computation | async-start | bytes 65536 | tf_op jit(solution)/shard_map/all_to_all | solution.py:225
  18.1 0.0 copy-done
  18.2 0.0 copy-done.2
  18.2 7.8 %all-gather = bf16[160,512]{1,0:T(8,128)(2,1)S(1)} all-gather(bf16[40,512]{1,0:T(8,128)(2,1)S(1)} %shard_map.59), channel_id=2, replica_groups={{258,259,0,1},{2,3,256,257},{262,263,4,5},{6,7,260,261},{266,267,8,9},{..., dimensions={0}, use_global_device_ids=true | all-gather | bytes 204800 | tf_op jit(solution)/shard_map/all_gather | solution.py:244
  26.0 0.0 all-to-all-done
  26.0 1.0 %shard_map.60 = (bf16[512,48]{1,0:T(8,128)(2,1)S(1)}, bf16[48,2048]{1,0:T(8,128)(2,1)S(1)}, f32[16,4,128]{2,1,0:T(4,128)S(1)}) custom-call(bf16[128,128]{1,0:T(8,128)(2,1)S(1)} %bitcast.9, bf16[4,40,512]{2,1,0:T(8,128)(2,1)S(1)} %bitcast.7), custom_call_target="tpu_custom_call" | custom-call | tf_op jit(solution)/shard_map/pallas_call | solution.py:230
  27.0 14.6 %all_to_all.20.rows_ref = f32[16,4,128]{2,1,0:T(4,128)S(1)} all-to-all(f32[16,4,128]{2,1,0:T(4,128)S(1)} %get-tuple-element.14), channel_id=1, replica_groups={{36,40,32,44,28,48,24,52,20,56,16,60,12,0,8,4},{37,41,33,45,29,49,25,53..., dimensions={0} | all-to-all | bytes 65536 | tf_op jit(solution)/shard_map/all_to_all | solution.py:225
  41.6 1.4 %shard_map.61 = (bf16[512,48]{1,0:T(8,128)(2,1)S(1)}, f32[1,128]{1,0:T(1,128)S(1)}, bf16[32,24,128]{2,1,0:T(8,128)(2,1)S(1)}, f32[1,32]{1,0:T(1,128)}) custom-call(bf16[512,48]{1,0:T(8,128)(2,1)S(1)} %get-tuple-element.12.x_ref, bf16[48,2048]{1,0:T(8,128)(2,1)S(1)} %get-tuple-element.13.y_ref, f32[16,4,128]{2,1,0:T(4,128)S(1)} %all_to_all.20.rows_ref), custom_call_target="tpu_custom_call" | custom-call | tf_op jit(solution)/shard_map/pallas_call | solution.py:230
  43.0 13.2 %all_to_all.21.cols_ref = bf16[32,24,128]{2,1,0:T(8,128)(2,1)S(1)} all-to-all(bf16[32,24,128]{2,1,0:T(8,128)(2,1)S(1)} %get-tuple-element.18), channel_id=1, replica_groups={{130,131,66,194,384,386,67,195,385,387,2,128,320,322,448,450,3,129,321,..., dimensions={0} | all-to-all | bytes 393216 | tf_op jit(solution)/shard_map/all_to_all | solution.py:225
  56.2 1.9 %shard_map.62 = (f32[144,128]{1,0:T(8,128)S(1)}, f32[4,128]{1,0:T(4,128)}) custom-call(bf16[512,48]{1,0:T(8,128)(2,1)S(1)} %get-tuple-element.16.x_ref, bf16[48,2048]{1,0:T(8,128)(2,1)S(1)} %get-tuple-element.13.y_ref, f32[1,128]{1,0:T(1,128)S(1)} %get-tuple-element.17.shift_ref, bf16[32,24,128]{2,1,0:T(8,128)(2,1)S(1)} %all_to_all.21.cols_ref), custom_call_target="tpu_custom_call" | custom-call | tf_op jit(solution)/shard_map/pallas_call | solution.py:230
  58.1 14.5 %all_to_all.22 = f32[16,9,1,128]{3,2,1,0:T(1,128)S(1)} all-to-all(f32[16,9,1,128]{3,2,1,0:T(1,128)S(1)} %bitcast.10), channel_id=1, replica_groups={{32,36,28,40,24,44,20,48,16,52,12,56,8,60,4,0},{33,37,29,41,25,45,21,49..., dimensions={0} | all-to-all | bytes 147456 | tf_op jit(solution)/shard_map/all_to_all | solution.py:225
  72.6 0.8 %shard_map.63 = f32[32,32]{1,0:T(8,128)} custom-call(f32[144,128]{1,0:T(8,128)S(1)} %bitcast.8), custom_call_target="tpu_custom_call" | custom-call | tf_op jit(solution)/shard_map/pallas_call | solution.py:230
  (1 shorter events, 0.0 us)
Async XLA Ops:
  0.6 0.7 copy-start.1
  2.1 16.1 %copy-start = (bf16[32,512]{1,0:T(8,128)(2,1)S(1)}, bf16[32,512]{1,0:T(8,128)(2,1)}, u32[]{:S(2)}) copy-start(bf16[32,512]{1,0:T(8,128)(2,1)} %samples_ref.1) | copy-start | bytes 98308
  2.1 16.1 %copy-start.2 = (f32[512]{0:T(512)S(1)}, f32[512]{0:T(512)}, u32[]{:S(2)}) copy-start(f32[512]{0:T(512)} %param.5) | copy-start | bytes 6148
  2.1 23.9 %all-to-all-start = ((bf16[16,8,128]{2,1,0:T(8,128)(2,1)}), bf16[16,8,128]{2,1,0:T(8,128)(2,1)S(1)}, u32[]{:S(2)}, u32[]{:S(2)}) async-start(bf16[16,8,128]{2,1,0:T(8,128)(2,1)} %shard_map.58), calls=%async_computation | async-start | bytes 65536 | tf_op jit(solution)/shard_map/all_to_all | solution.py:225

commit v12 on v10

--- a/solution.py
+++ b/solution.py
@@ -218,7 +218,7 @@
 Z_ORDER = (12, 13, 11, 14, 10, 15, 9, 0, 8, 1, 7, 2, 6, 3, 5, 4)
 Z_ROWS = (9, 10, 8, 11, 7, 12, 6, 13, 5, 14, 4, 15, 3, 0, 2, 1)
 Z_PARTS = (8, 9, 7, 10, 6, 11, 5, 12, 4, 13, 3, 14, 2, 15, 1, 0)
-PLANE_ORDER = (10, 11, 6, 14, 24, 26, 7, 15, 25, 27, 2, 8, 20, 22, 28, 30, 3, 9, 21, 23, 29, 31, 4, 12, 16, 18, 5, 13, 17, 19, 0, 1)
+PLANE_ORDER = (11, 10, 7, 15, 25, 27, 6, 14, 24, 26, 3, 9, 21, 23, 29, 31, 2, 8, 20, 22, 28, 30, 5, 13, 17, 19, 4, 12, 16, 18, 1, 0)
 
 
 def exchange(value, axes, order):

time: 74.2 us -> 73.8 us (level)
  no operation moved by 1% of the time
where the time goes in v12:
time: 73.8 us; the launch traced here: 73.5 us
  blocking collectives  50.2 us (68%)
  starting transfers between devices  16.1 us (22%)
  Pallas kernels  5.82 us (8%)
    all_to_all x3, blocking collectives, exchange(): return lax.all_to_all(value, axes, 0, 0, axis_index_groups=[list(order)])  42.4 us
    all_to_all x1, starting transfers between devices, exchange(): return lax.all_to_all(value, axes, 0, 0, axis_index_groups=[list(order)])  16.1 us
    all_gather x1, blocking collectives, on_device(): ys = lax.all_gather(own, ('x_lo', 'x_hi', 'core'), axis_index_groups=near)  7.8 us
    pallas_call x6, Pallas kernels, call(): pl.pallas_call(body, out_shape=[jax.ShapeDtypeStruct(shape, dtype) for sh...  5.82 us
  transfers between devices with their start and end apart: 1, of which 0 were waited for; matrix products, arithmetic and copies ran while one was open for 0% of the time, Pallas kernels for 0%

profile of v12, /device:TPU:1, one launch (start us, length us, event | category | flops | bytes accessed | tf_op | source)
XLA Modules:
  0.0 73.5 jit_solution(1320111906062285541)
XLA Ops:
  0.6 0.0 copy-start.1
  0.6 0.7 copy-done.1
  1.3 0.7 %shard_map.58 = bf16[16,8,128]{2,1,0:T(8,128)(2,1)} custom-call(bf16[32,32]{1,0:T(8,128)(2,1)S(1)} %copy-done.1), custom_call_target="tpu_custom_call" | custom-call | tf_op jit(solution)/shard_map/pallas_call | solution.py:230
  2.1 0.0 copy-start
  2.1 0.0 copy-start.2
  2.1 16.1 %all-to-all-start = ((bf16[16,8,128]{2,1,0:T(8,128)(2,1)}), bf16[16,8,128]{2,1,0:T(8,128)(2,1)S(1)}, u32[]{:S(2)}, u32[]{:S(2)}) async-start(bf16[16,8,128]{2,1,0:T(8,128)(2,1)} %shard_map.58), calls=%async_computation | async-start | bytes 65536 | tf_op jit(solution)/shard_map/all_to_all | solution.py:225
  18.1 0.0 copy-done
  18.2 0.0 copy-done.2
  18.2 7.8 %all-gather = bf16[160,512]{1,0:T(8,128)(2,1)S(1)} all-gather(bf16[40,512]{1,0:T(8,128)(2,1)S(1)} %shard_map.59), channel_id=2, replica_groups={{0,1,258,259},{256,257,2,3},{4,5,262,263},{260,261,6,7},{8,9,266,267},{..., dimensions={0}, use_global_device_ids=true | all-gather | bytes 204800 | tf_op jit(solution)/shard_map/all_gather | solution.py:244
  26.0 0.0 all-to-all-done
  26.0 1.0 %shard_map.60 = (bf16[512,48]{1,0:T(8,128)(2,1)S(1)}, bf16[48,2048]{1,0:T(8,128)(2,1)S(1)}, f32[16,4,128]{2,1,0:T(4,128)S(1)}) custom-call(bf16[128,128]{1,0:T(8,128)(2,1)S(1)} %bitcast.9, bf16[4,40,512]{2,1,0:T(8,128)(2,1)S(1)} %bitcast.7), custom_call_target="tpu_custom_call" | custom-call | tf_op jit(solution)/shard_map/pallas_call | solution.py:230
  27.0 14.6 %all_to_all.20.rows_ref = f32[16,4,128]{2,1,0:T(4,128)S(1)} all-to-all(f32[16,4,128]{2,1,0:T(4,128)S(1)} %get-tuple-element.14), channel_id=1, replica_groups={{36,40,32,44,28,48,24,52,20,56,16,60,12,0,8,4},{37,41,33,45,29,49,25,53..., dimensions={0} | all-to-all | bytes 65536 | tf_op jit(solution)/shard_map/all_to_all | solution.py:225
  41.6 1.4 %shard_map.61 = (bf16[512,48]{1,0:T(8,128)(2,1)S(1)}, f32[1,128]{1,0:T(1,128)S(1)}, bf16[32,24,128]{2,1,0:T(8,128)(2,1)S(1)}, f32[1,32]{1,0:T(1,128)}) custom-call(bf16[512,48]{1,0:T(8,128)(2,1)S(1)} %get-tuple-element.12.x_ref, bf16[48,2048]{1,0:T(8,128)(2,1)S(1)} %get-tuple-element.13.y_ref, f32[16,4,128]{2,1,0:T(4,128)S(1)} %all_to_all.20.rows_ref), custom_call_target="tpu_custom_call" | custom-call | tf_op jit(solution)/shard_map/pallas_call | solution.py:230
  43.0 13.0 %all_to_all.21.cols_ref = bf16[32,24,128]{2,1,0:T(8,128)(2,1)S(1)} all-to-all(bf16[32,24,128]{2,1,0:T(8,128)(2,1)S(1)} %get-tuple-element.18), channel_id=1, replica_groups={{131,130,67,195,385,387,66,194,384,386,3,129,321,323,449,451,2,128,320,..., dimensions={0} | all-to-all | bytes 393216 | tf_op jit(solution)/shard_map/all_to_all | solution.py:225
  56.0 1.9 %shard_map.62 = (f32[144,128]{1,0:T(8,128)S(1)}, f32[4,128]{1,0:T(4,128)}) custom-call(bf16[512,48]{1,0:T(8,128)(2,1)S(1)} %get-tuple-element.16.x_ref, bf16[48,2048]{1,0:T(8,128)(2,1)S(1)} %get-tuple-element.13.y_ref, f32[1,128]{1,0:T(1,128)S(1)} %get-tuple-element.17.shift_ref, bf16[32,24,128]{2,1,0:T(8,128)(2,1)S(1)} %all_to_all.21.cols_ref), custom_call_target="tpu_custom_call" | custom-call | tf_op jit(solution)/shard_map/pallas_call | solution.py:230
  57.9 14.8 %all_to_all.22 = f32[16,9,1,128]{3,2,1,0:T(1,128)S(1)} all-to-all(f32[16,9,1,128]{3,2,1,0:T(1,128)S(1)} %bitcast.10), channel_id=1, replica_groups={{32,36,28,40,24,44,20,48,16,52,12,56,8,60,4,0},{33,37,29,41,25,45,21,49..., dimensions={0} | all-to-all | bytes 147456 | tf_op jit(solution)/shard_map/all_to_all | solution.py:225
  72.7 0.8 %shard_map.63 = f32[32,32]{1,0:T(8,128)} custom-call(f32[144,128]{1,0:T(8,128)S(1)} %bitcast.8), custom_call_target="tpu_custom_call" | custom-call | tf_op jit(solution)/shard_map/pallas_call | solution.py:230
  (1 shorter events, 0.0 us)
Async XLA Ops:
  0.6 0.7 copy-start.1
  2.1 16.1 %copy-start = (bf16[32,512]{1,0:T(8,128)(2,1)S(1)}, bf16[32,512]{1,0:T(8,128)(2,1)}, u32[]{:S(2)}) copy-start(bf16[32,512]{1,0:T(8,128)(2,1)} %samples_ref.1) | copy-start | bytes 98308
  2.1 16.1 %copy-start.2 = (f32[512]{0:T(512)S(1)}, f32[512]{0:T(512)}, u32[]{:S(2)}) copy-start(f32[512]{0:T(512)} %param.5) | copy-start | bytes 6148
  2.1 23.9 %all-to-all-start = ((bf16[16,8,128]{2,1,0:T(8,128)(2,1)}), bf16[16,8,128]{2,1,0:T(8,128)(2,1)S(1)}, u32[]{:S(2)}, u32[]{:S(2)}) async-start(bf16[16,8,128]{2,1,0:T(8,128)(2,1)} %shard_map.58), calls=%async_computation | async-start | bytes 65536 | tf_op jit(solution)/shard_map/all_to_all | solution.py:225
